TPU v7x, 256 devices: a whole 4x4x8 slice. The times are simulated.
256 devices in a mesh: dp: 16 (over x, y), tensor: 16 (over z, core).
Axes of the slice: x: 4, y: 4, z: 8, core: 2. Of those that a mesh axis runs over, the one named last changes fastest.
Arguments:
- hidden: bfloat16 [32768, 1280], P(('dp', 'tensor')), may hold values from -6 to 6
- lengths: int32 [16, 8], P('dp'), may hold values from 1 to 1024, 2048 in all within a row
- request_prompt: int32 [16, 8], P('dp'), may hold values from 0 to 31
- request_adapter: int32 [16, 8], P('dp'), may hold values from 0 to 63
- prompt_page_table: int32 [32, 4], replicated, may hold values from 0 to 63
- prefix_page_cache: bfloat16 [64, 64, 2048], P('dp', None, 'tensor'), may hold values from -6 to 6
- query_key_value_weight: bfloat16 [1280, 3072], P(None, 'tensor'), may hold values from -0.15625 to 0.15625
- adapter_down: bfloat16 [64, 1280, 16], P('dp'), may hold values from -0.15625 to 0.15625
- adapter_up: bfloat16 [64, 16, 3072], P('dp', None, 'tensor'), may hold values from -1.5 to 1.5
- attention_scale: float32 [1024], P('tensor'), may hold values from 0.5 to 1.5
- output_matrix: bfloat16 [1024, 1280], P('tensor'), may hold values from -0.1875 to 0.1875
- attention_rate: float32 [1280], replicated, may hold values from 0.05 to 0.5
- up_matrix: bfloat16 [1280, 5120], P(None, 'tensor'), may hold values from -0.15625 to 0.15625
- gate_matrix: bfloat16 [1280, 5120], P(None, 'tensor'), may hold values from -0.15625 to 0.15625
- up_scaling: float32 [5120], P('tensor'), may hold values from 0.5 to 2
- gate_scaling: float32 [5120], P('tensor'), may hold values from 0.5 to 2
- down_matrix: bfloat16 [5120, 1280], P('tensor'), may hold values from -0.078125 to 0.078125
- feedforward_rate: float32 [1280], replicated, may hold values from 0.05 to 0.5
Outputs:
- hidden_out: bfloat16 [32768, 1280], P(('dp', 'tensor'))
Inputs may be any that keep to these rules, and one draw needn't show every extreme that they name: Each group's lengths sum to 2048.
All inputs are finite; a program needn't handle non-finite values.
Results may differ from a plain program's by a relative error of at most 0.015.
Values may be sent and summed in bfloat16 or wider, within the bound.
A program may use at most 64 MiB of HBM per device.

v0:
```python
import math

import jax
import jax.numpy as jnp
from jax import lax
from jax.sharding import PartitionSpec as P

MODEL_WIDTH = 1280
HEAD_WIDTH = 64
ADAPTER_RANK = 16
GROUP_REQUESTS = 8
PAGE = 64
PREFIX_LEN = 256


adapter_scale = 0.5
epsilon = 1e-06


def renorm(matrix):
    return matrix * lax.rsqrt(jnp.mean(matrix * matrix, axis=-1, keepdims=True) + epsilon)


def to_unit(vectors):
    return vectors * lax.rsqrt(jnp.sum(vectors * vectors, axis=-1, keepdims=True) + epsilon)


def rotate(vectors, position):
    half_size = vectors.shape[-1] // 2
    frequency = jnp.exp(
        jnp.arange(half_size).astype(jnp.float32) * (-2.0 * math.log(10000.0) / vectors.shape[-1])
    )
    angles = position[:, None] * frequency[None, :]
    cosine = jnp.cos(angles)[:, None, :]
    sines = jnp.sin(angles)[:, None, :]
    first_half = vectors[..., :half_size]
    second_half = vectors[..., half_size:]
    return jnp.concatenate(
        [first_half * cosine - second_half * sines, first_half * sines + second_half * cosine],
        axis=-1,
    )


def layout(counts, total_rows):
    row_ends = jnp.cumsum(counts)
    starts = row_ends - counts
    row_ids = jnp.arange(total_rows, dtype=jnp.int32)
    request_number = jnp.sum((row_ids[:, None] >= row_ends[None, :]).astype(jnp.int32), axis=1)
    selected_adapter = (
        request_number[:, None] == jnp.arange(counts.shape[0], dtype=jnp.int32)[None, :]
    )
    offset = row_ids - jnp.sum(jnp.where(selected_adapter, starts[None, :], 0), axis=1)
    return (request_number, offset)


def attend(queries, key_all, value_all, request_number, key_request, key_row):
    rows_total = queries.shape[0]
    block_rows = min(512, rows_total)
    score_scale = math.sqrt(queries.shape[-1])
    row_ids = jnp.arange(rows_total, dtype=jnp.int32)

    def one_block(block_index):
        first_row = block_index * block_rows
        query_block = lax.dynamic_slice_in_dim(queries, first_row, block_rows, 0)
        request_block = lax.dynamic_slice_in_dim(request_number, first_row, block_rows, 0)
        row_block = lax.dynamic_slice_in_dim(row_ids, first_row, block_rows, 0)
        scores = (
            jnp.einsum("qhd,khd->hqk", query_block, key_all, preferred_element_type=jnp.float32)
            * score_scale
        )
        allowed = (request_block[:, None] == key_request[None, :]) & (
            key_row[None, :] <= row_block[:, None]
        )
        exp_scores = jnp.where(allowed[None], jnp.exp(scores), 0.0)
        weights = (exp_scores / jnp.sum(exp_scores, axis=-1, keepdims=True)).astype(jnp.bfloat16)
        mixed_block = jnp.einsum(
            "hqk,khd->qhd", weights, value_all, preferred_element_type=jnp.float32
        )
        return mixed_block.reshape(block_rows, -1).astype(jnp.bfloat16)

    blocks = lax.map(one_block, jnp.arange(rows_total // block_rows, dtype=jnp.int32))
    return blocks.reshape(rows_total, -1)


def hidden_units(row_values, up_matrix, gate_matrix, up_scaling, gate_scaling):
    up_part = jnp.dot(row_values, up_matrix, preferred_element_type=jnp.float32) * up_scaling
    gate_part = jnp.dot(row_values, gate_matrix, preferred_element_type=jnp.float32) * gate_scaling
    return (up_part * jax.nn.silu(gate_part)).astype(jnp.bfloat16)


def local(
    hidden,
    lengths,
    request_prompt,
    request_adapter,
    prompt_page_table,
    prefix_page_cache,
    query_key_value_weight,
    adapter_down,
    adapter_up,
    attention_scale,
    output_matrix,
    attention_rate,
    up_matrix,
    gate_matrix,
    up_scaling,
    gate_scaling,
    down_matrix,
    feedforward_rate,
):
    tok_rows = hidden.shape[0]
    group_rows = tok_rows * lax.axis_size("tensor")
    heads_here = query_key_value_weight.shape[1] // (3 * HEAD_WIDTH)
    gain_qk = attention_scale.reshape(heads_here, HEAD_WIDTH)
    request_number, offset = layout(lengths[0], group_rows)
    position = offset.astype(jnp.float32) + PREFIX_LEN
    local_cache = prefix_page_cache.reshape(
        prefix_page_cache.shape[0], PAGE, heads_here, 2, HEAD_WIDTH
    )
    local_keys = (to_unit(local_cache[:, :, :, 0, :].astype(jnp.float32)) * gain_qk).astype(
        jnp.bfloat16
    )
    prepared = jnp.stack([local_keys, local_cache[:, :, :, 1, :]], axis=3).reshape(
        prefix_page_cache.shape
    )
    all_pages = lax.all_gather(prepared, "dp", axis=0, tiled=True)
    down_all, up_all = (
        lax.all_gather(adapter_down, "dp", axis=0, tiled=True),
        lax.all_gather(adapter_up, "dp", axis=0, tiled=True),
    )
    every_row = lax.all_gather(hidden, "tensor", axis=0, tiled=True)
    adapter_count = down_all.shape[0]
    onehot = (
        request_adapter[0][:, None] == jnp.arange(adapter_count, dtype=jnp.int32)[None, :]
    ).astype(jnp.bfloat16)
    selected_down = jnp.dot(
        onehot, down_all.reshape(adapter_count, -1), preferred_element_type=jnp.float32
    ).astype(jnp.bfloat16)
    selected_down = jnp.transpose(
        selected_down.reshape(GROUP_REQUESTS, MODEL_WIDTH, ADAPTER_RANK), (1, 0, 2)
    ).reshape(MODEL_WIDTH, GROUP_REQUESTS * ADAPTER_RANK)
    selected_up = jnp.dot(
        onehot, up_all.reshape(adapter_count, -1), preferred_element_type=jnp.float32
    ).astype(jnp.bfloat16)
    selected_up = selected_up.reshape(GROUP_REQUESTS * ADAPTER_RANK, heads_here * 3 * HEAD_WIDTH)
    request_of_slot = jnp.arange(GROUP_REQUESTS * ADAPTER_RANK, dtype=jnp.int32) // ADAPTER_RANK
    plain_projection = jnp.dot(
        every_row, query_key_value_weight, preferred_element_type=jnp.float32
    )
    adapter_middle = jnp.dot(every_row, selected_down, preferred_element_type=jnp.float32)
    adapter_middle = jnp.where(
        request_number[:, None] == request_of_slot[None, :], adapter_middle, 0.0
    ).astype(jnp.bfloat16)
    query_key_value = (
        plain_projection
        + adapter_scale * jnp.dot(adapter_middle, selected_up, preferred_element_type=jnp.float32)
    ).reshape(group_rows, heads_here, 3, HEAD_WIDTH)
    queries = (to_unit(rotate(query_key_value[:, :, 0, :], position)) * gain_qk).astype(
        jnp.bfloat16
    )
    key_own = (to_unit(rotate(query_key_value[:, :, 1, :], position)) * gain_qk).astype(
        jnp.bfloat16
    )
    value_own = query_key_value[:, :, 2, :].astype(jnp.bfloat16)
    page_list = prompt_page_table[request_prompt[0]].reshape(-1)
    picked = jnp.take(all_pages, page_list, axis=0).reshape(
        GROUP_REQUESTS * PREFIX_LEN, heads_here, 2, HEAD_WIDTH
    )
    key_all = jnp.concatenate([picked[:, :, 0, :], key_own], axis=0)
    value_all = jnp.concatenate([picked[:, :, 1, :], value_own], axis=0)
    key_request = jnp.concatenate(
        [jnp.arange(GROUP_REQUESTS * PREFIX_LEN, dtype=jnp.int32) // PREFIX_LEN, request_number],
        axis=0,
    )
    key_row = jnp.concatenate(
        [
            jnp.full((GROUP_REQUESTS * PREFIX_LEN,), -1, jnp.int32),
            jnp.arange(group_rows, dtype=jnp.int32),
        ],
        axis=0,
    )
    attn = attend(queries, key_all, value_all, request_number, key_request, key_row)
    attn_sum = lax.psum_scatter(
        jnp.dot(attn, output_matrix, preferred_element_type=jnp.float32).astype(jnp.bfloat16),
        "tensor",
        scatter_dimension=0,
        tiled=True,
    ).astype(jnp.float32)
    base_rows = hidden.astype(jnp.float32)
    mixed = renorm(base_rows + attention_rate * (renorm(attn_sum) - base_rows)).astype(jnp.bfloat16)
    unit_values = hidden_units(
        lax.all_gather(mixed, "tensor", axis=0, tiled=True),
        up_matrix,
        gate_matrix,
        up_scaling,
        gate_scaling,
    )
    mlp_sum = lax.psum_scatter(
        jnp.dot(unit_values, down_matrix, preferred_element_type=jnp.float32).astype(jnp.bfloat16),
        "tensor",
        scatter_dimension=0,
        tiled=True,
    ).astype(jnp.float32)
    mixed_rows = mixed.astype(jnp.float32)
    return renorm(mixed_rows + feedforward_rate * (renorm(mlp_sum) - mixed_rows)).astype(
        jnp.bfloat16
    )


def solution(mesh):
    placed = (
        P(("dp", "tensor"), None),
        P("dp", None),
        P("dp", None),
        P("dp", None),
        P(),
        P("dp", None, "tensor"),
        P(None, "tensor"),
        P("dp", None, None),
        P("dp", None, "tensor"),
        P("tensor"),
        P("tensor", None),
        P(),
        P(None, "tensor"),
        P(None, "tensor"),
        P("tensor"),
        P("tensor"),
        P("tensor", None),
        P(),
    )
    return jax.shard_map(
        local, mesh=mesh, in_specs=placed, out_specs=P(("dp", "tensor"), None), check_vma=False
    )
```

profile of v0, /device:TPU:1, one launch (start us, length us, event | category | flops | bytes accessed | tf_op | source)
XLA Modules:
  0.0 395.4 jit_solution(10989033186772423542)
XLA Ops:
  6.5 1.0 reshape.596
  7.6 0.6 multiply_reduce_fusion.4
  8.2 0.1 slice.53
  8.3 1.0 multiply_convert_fusion.4
  9.3 0.4 pad_maximum_fusion.4
  9.7 0.7 reshape.597
  10.5 0.7 all-gather.7.cloned.1.call-update
  11.3 0.7 all-gather.5.cloned.1.call-update
  12.0 0.8 copy.41
  12.8 0.7 fusion.40
  13.4 0.6 gather_fusion
  14.0 0.1 reshape.598
  14.1 0.1 reshape.595
  14.1 0.8 reduce-window.4
  15.0 20.5 %all_gather.17 = bf16[64,16,192]{2,1,0:T(8,128)(2,1)S(1)} all-gather(bf16[4,16,192]{2,1,0:T(8,128)(2,1)} %param.28), channel_id=1, replica_groups=mesh['dp'=16,'tensor'=16] {'dp'}, dimensions={0}, use_global_device_ids=true | all-gather | bytes 417792 | tf_op jit(solution)/shard_map/all_gather | solution.py:129
  35.5 0.5 reshape.591
  36.0 0.9 convolution_convert_fusion.3
  36.9 0.1 reshape.592
  37.1 0.1 broadcast_in_dim.45
  37.3 0.1 convert_reduce_fusion
  37.4 0.7 fusion.42
  38.0 0.1 select_reduce_fusion
  38.1 22.6 %all-gather.9.cloned.1.call-done = bf16[64,64,128]{2,1,0:T(8,128)(2,1)} async-done(((bf16[4,64,128]{2,1,0:T(8,128)(2,1)}), bf16[64,64,128]{2,1,0:T(8,128)(2,1)}) %all-gather.9.cloned.1.call-update) | async-done | bytes 1048592 | tf_op jit(solution)/shard_map/all_gather | solution.py:126
  60.7 1.9 gather_fusion.1
  62.6 0.4 reshape.616
  63.0 0.9 copy.44
  64.0 0.9 slice_bitcast_fusion.2
  64.9 50.0 %all-gather.7.cloned.1.call-done = bf16[64,1280,16]{1,2,0:T(8,128)(2,1)} async-done(((bf16[4,1280,16]{1,2,0:T(8,128)(2,1)}), bf16[64,1280,16]{1,2,0:T(8,128)(2,1)}) %all-gather.7.cloned.1.call-update) | async-done | bytes 2621456 | tf_op jit(solution)/shard_map/all_gather | solution.py:128
  114.9 9.7 %copy.39 = bf16[64,1280,16]{0,2,1:T(8,128)(2,1)} copy(bf16[64,1280,16]{1,2,0:T(8,128)(2,1)} %all-gather.7.cloned.1.call-done) | data formatting | bytes 5242880 | tf_op jit(solution)/shard_map/all_gather | solution.py:128
  124.6 4.7 %convolution_convert_fusion = bf16[8,20480]{1,0:T(8,128)(2,1)} fusion(bf16[64,20480]{0,1:T(8,128)(2,1)} %bitcast.89, s32[8]{0:T(128)S(1)} %bitcast.97), kind=kOutput, calls=%fused_computation.13 | convolution fusion | flops 21135872 | bytes 2949152 | tf_op jit(solution)/shard_map/dot_general | solution.py:136
  129.3 2.9 reshape.589
  132.2 1.6 copy.40
  133.8 26.4 %all-gather.5.cloned.1.call-done = bf16[2048,1280]{1,0:T(8,128)(2,1)} async-done(((bf16[128,1280]{1,0:T(8,128)(2,1)}), bf16[2048,1280]{1,0:T(8,128)(2,1)}) %all-gather.5.cloned.1.call-update) | async-done | bytes 5242896 | tf_op jit(solution)/shard_map/all_gather | solution.py:131
  160.2 5.6 %fusion.46 = f32[2048,192]{0,1:T(8,128)} fusion(bf16[2048,1280]{1,0:T(8,128)(2,1)} %all-gather.5.cloned.1.call-done, bf16[1280,192]{0,1:T(8,128)(2,1)} %param.26), kind=kOutput, calls=%fused_computation.120 | convolution fusion | flops 1006632960 | bytes 7307264 | tf_op jit(solution)/shard_map/dot_general | solution.py:147
  165.9 5.0 %fusion.11 = f32[2048,192]{0,1:T(8,128)S(1)} fusion(f32[2048,192]{0,1:T(8,128)} %fusion.46, bf16[128,192]{1,0:T(8,128)(2,1)S(1)} %reshape.592, bf16[1280,128]{0,1:T(8,128)(2,1)S(1)} %bitcast.94, bf16[2048,1280]{1,0:T(8,128)(2,1)} %all-gather.5.cloned.1.call-done, s32[2048]{0:T(1024)S(1)} %convert_reduce_fusion, s32[128]{0:T(128)S(1)} %and_select_fusion), kind=kOutput, calls=%fused_computation.22 | convolution fusion | flops 773324800 | bytes 8774144 | tf_op jit(solution)/shard_map/dot_general | solution.py:156
  171.0 1.2 fusion.32
  172.3 0.1 multiply_reduce_fusion.2
  172.4 0.2 multiply_convert_fusion.2
  172.8 22.6 %while.11 = (s32[]{:T(128)}, bf16[4,512,64]{1,2,0:T(8,128)(2,1)S(1)}, s32[4]{0:T(128)S(1)}, s32[2048]{0:T(1024)S(1)}, s32[4096]{0:T(1024)S(1)}, /*index=5*/s32[2...) while((s32[]{:T(128)}, ...), condition=%wide.region_8.9_spmd, body=%wide.region_6.8_spmd.sunk | while | flops 553680384 | bytes 18006224 | solution.py:81
  172.8 0.6 dynamic_slice.32
  174.0 0.1 dynamic_slice.33
  174.2 2.7 fusion.65
  176.9 1.5 fusion.66
  178.4 0.6 dynamic_slice.32
  179.8 2.7 fusion.65
  182.5 1.5 fusion.66
  184.0 0.6 dynamic_slice.32
  185.4 2.7 fusion.65
  188.1 1.5 fusion.66
  189.6 0.6 dynamic_slice.32
  191.0 2.7 fusion.65
  193.7 1.5 fusion.66
  195.4 3.9 convolution_convert_fusion.2
  199.4 59.8 %reduce-scatter.3.cloned.1.call-done = bf16[128,1280]{1,0:T(8,128)(2,1)} async-done(((bf16[2048,1280]{1,0:T(8,128)(2,1)}), bf16[128,1280]{1,0:T(8,128)(2,1)}) %reduce-scatter.3.cloned.1.call-update) | async-done | bytes 327696 | tf_op jit(solution)/shard_map/reduce_scatter | solution.py:183
  259.2 1.1 fusion.16
  260.3 1.3 multiply_reduce_fusion.1
  261.6 2.1 multiply_convert_fusion.1
  263.8 45.7 %all-gather.11.cloned.1.call-done = bf16[2048,1280]{1,0:T(8,128)(2,1)} async-done(((bf16[128,1280]{1,0:T(8,128)(2,1)}), bf16[2048,1280]{1,0:T(8,128)(2,1)}) %all-gather.11.cloned.1.call-update) | async-done | bytes 5242896 | tf_op jit(solution)/shard_map/all_gather | solution.py:192
  309.6 5.9 %convolution_multiply_fusion = f32[2048,320]{0,1:T(8,128)} fusion(bf16[2048,1280]{1,0:T(8,128)(2,1)} %all-gather.11.cloned.1.call-done, bf16[1280,320]{0,1:T(8,128)(2,1)S(1)} %copy-done.12, f32[320]{0:T(512)S(1)} %copy-done.14), kind=kOutput, calls=%fused_computation.17 | convolution fusion | flops 1678376960 | bytes 8684800 | tf_op jit(solution)/shard_map/dot_general | solution.py:87
  315.5 8.7 %convolution_convert_fusion.1 = bf16[2048,1280]{1,0:T(8,128)(2,1)} fusion(bf16[320,1280]{1,0:T(8,128)(2,1)S(1)} %copy-done, bf16[2048,1280]{1,0:T(8,128)(2,1)} %all-gather.11.cloned.1.call-done, bf16[1280,320]{0,1:T(8,128)(2,1)S(1)} %copy-done.13, f32[2048,320]{0,1:T(8,128)} %convolution_multiply_fusion, f32[320]{0:T(512)S(1)} %copy-done.15), kind=kOutput, calls=%fused_computation.14 | convolution fusion | flops 3362652160 | bytes 14746880 | tf_op jit(solution)/shard_map/dot_general | solution.py:199
  324.2 59.8 %reduce-scatter.5.cloned.1.call-done = bf16[128,1280]{1,0:T(8,128)(2,1)} async-done(((bf16[2048,1280]{1,0:T(8,128)(2,1)}), bf16[128,1280]{1,0:T(8,128)(2,1)}) %reduce-scatter.5.cloned.1.call-update) | async-done | bytes 327696 | tf_op jit(solution)/shard_map/reduce_scatter | solution.py:198
  384.0 1.1 fusion.18
  385.2 1.3 multiply_reduce_fusion
  386.5 2.1 multiply_convert_fusion
  (77 shorter events, 1.3 us)
Async XLA Ops:
  6.5 308.9 %copy-start = (bf16[320,1280]{1,0:T(8,128)(2,1)S(1)}, bf16[320,1280]{1,0:T(8,128)(2,1)}, u32[]{:S(2)}) copy-start(bf16[320,1280]{1,0:T(8,128)(2,1)} %param.36) | copy-start | bytes 2457604
  6.5 54.2 %all-gather.9.cloned.1.call-start = ((), (), s32[]{:S(2)}) async-start(), calls=%async_computation.4 | async-start | bytes 1114112 | tf_op jit(solution)/shard_map/all_gather | solution.py:126
  10.5 104.4 %all-gather.7.cloned.1.call-start = ((), (), s32[]{:S(2)}) async-start(), calls=%async_computation.3 | async-start | bytes 2785280 | tf_op jit(solution)/shard_map/all_gather | solution.py:128
  11.2 149.0 %all-gather.5.cloned.1.call-start = ((), (), s32[]{:S(2)}) async-start(), calls=%async_computation.2 | async-start | bytes 5570560 | tf_op jit(solution)/shard_map/all_gather | solution.py:131
  12.0 247.2 %reduce-scatter.3.cloned.1.call-start = ((), (), s32[]{:S(2)}) async-start(), calls=%async_computation.5 | async-start | bytes 5570560 | tf_op jit(solution)/shard_map/reduce_scatter | solution.py:183
  63.9 60.7 %copy-start.11 = (s32[1,8]{1,0:T(1,128)S(1)}, s32[1,8]{1,0:T(1,128)}, u32[]{:S(2)}) copy-start(s32[1,8]{1,0:T(1,128)} %param.23) | copy-start | bytes 100
  133.8 32.0 %copy-start.3 = (bf16[1280,8,16]{0,2,1:T(8,128)(2,1)S(1)}, bf16[1280,8,16]{0,2,1:T(8,128)(2,1)}, u32[]{:S(2)}) copy-start(bf16[1280,8,16]{0,2,1:T(8,128)(2,1)} %copy.40) | copy-start | bytes 983044
  165.9 6.5 %copy-start.10 = (f32[64]{0:T(128)S(1)}, f32[64]{0:T(128)}, u32[]{:S(2)}) copy-start(f32[64]{0:T(128)} %param.29) | copy-start | bytes 772
  170.9 1.7 copy-start.5
  170.9 1.8 copy-start.4
  170.9 1.8 copy-start.6
  170.9 1.8 copy-start.16
  172.8 22.7 %copy-start.7 = (bf16[64,1280]{1,0:T(8,128)(2,1)S(1)}, bf16[64,1280]{1,0:T(8,128)(2,1)}, u32[]{:S(2)}) copy-start(bf16[64,1280]{1,0:T(8,128)(2,1)} %param.30) | copy-start | bytes 491524
  199.3 61.0 %copy-start.2 = (bf16[128,1280]{1,0:T(8,128)(2,1)S(1)}, bf16[128,1280]{1,0:T(8,128)(2,1)}, u32[]{:S(2)}) copy-start(bf16[128,1280]{1,0:T(8,128)(2,1)} %param.20) | copy-start | bytes 983044
  199.3 61.0 %copy-start.8 = (f32[1280]{0:T(1024)S(1)}, f32[1280]{0:T(1024)}, u32[]{:S(2)}) copy-start(f32[1280]{0:T(1024)} %param.31) | copy-start | bytes 15364
  199.3 110.3 %copy-start.12 = (bf16[1280,320]{0,1:T(8,128)(2,1)S(1)}, bf16[1280,320]{0,1:T(8,128)(2,1)}, u32[]{:S(2)}) copy-start(bf16[1280,320]{0,1:T(8,128)(2,1)} %param.33) | copy-start | bytes 2457604
  199.3 110.3 %copy-start.14 = (f32[320]{0:T(512)S(1)}, f32[320]{0:T(512)}, u32[]{:S(2)}) copy-start(f32[320]{0:T(512)} %param.35) | copy-start | bytes 3844
  199.3 110.2 %all-gather.11.cloned.1.call-start = ((), (), s32[]{:S(2)}) async-start(), calls=%async_computation.6 | async-start | bytes 5570560 | tf_op jit(solution)/shard_map/all_gather | solution.py:192
  263.7 51.7 %copy-start.13 = (bf16[1280,320]{0,1:T(8,128)(2,1)S(1)}, bf16[1280,320]{0,1:T(8,128)(2,1)}, u32[]{:S(2)}) copy-start(bf16[1280,320]{0,1:T(8,128)(2,1)} %param.32) | copy-start | bytes 2457604
  263.8 51.7 %copy-start.15 = (f32[320]{0:T(512)S(1)}, f32[320]{0:T(512)}, u32[]{:S(2)}) copy-start(f32[320]{0:T(512)} %param.34) | copy-start | bytes 3844
  263.8 120.2 %reduce-scatter.5.cloned.1.call-start = ((), (), s32[]{:S(2)}) async-start(), calls=%async_computation.7 | async-start | bytes 5570560 | tf_op jit(solution)/shard_map/reduce_scatter | solution.py:198
  324.2 61.0 %copy-start.1 = (bf16[128,1280]{1,0:T(8,128)(2,1)S(1)}, bf16[128,1280]{1,0:T(8,128)(2,1)}, u32[]{:S(2)}) copy-start(bf16[128,1280]{1,0:T(8,128)(2,1)} %multiply_convert_fusion.1) | copy-start | bytes 983044
  324.2 61.0 %copy-start.9 = (f32[1280]{0:T(1024)S(1)}, f32[1280]{0:T(1024)}, u32[]{:S(2)}) copy-start(f32[1280]{0:T(1024)} %param.37) | copy-start | bytes 15364
Sparse Core Ops, SparseCore 0:
  10.6 50.0 all-gather.8
  63.2 51.6 all-gather.6
  116.7 43.4 all-gather.4
  199.5 59.6 reduce-scatter.2
  263.9 45.6 all-gather.10
  324.3 59.6 reduce-scatter.4
where the time goes:
time: 399 us; the launch traced here: 395 us
  waiting for transfers between devices  266 us (67%)
  matrix products  51.4 us (13%)
  local copies, waits for them, and re-layouts  25.6 us (6%)
  blocking collectives  20.5 us (5%)
  other arithmetic  15.1 us (4%)
  between operations  13.9 us (3%)
    reduce_scatter x1, waiting for transfers between devices, local(): lax.psum_scatter(jnp.dot(unit_values, down_matrix, preferred_element_type...  59.8 us
    reduce_scatter x1, waiting for transfers between devices, local(): lax.psum_scatter(jnp.dot(attn, output_matrix, preferred_element_type=jnp....  59.8 us
    all_gather x1, waiting for transfers between devices, local(): lax.all_gather(adapter_down, 'dp', axis=0, tiled=True)  50 us
    all_gather x1, waiting for transfers between devices, local(): lax.all_gather(mixed, 'tensor', axis=0, tiled=True)  45.7 us
    all_gather x1, waiting for transfers between devices, local(): every_row = lax.all_gather(hidden, 'tensor', axis=0, tiled=True)  26.4 us
    all_gather x1, waiting for transfers between devices, local(): all_pages = lax.all_gather(prepared, 'dp', axis=0, tiled=True)  22.6 us
    all_gather x1, blocking collectives, local(): lax.all_gather(adapter_up, 'dp', axis=0, tiled=True)  20.5 us
    dot_general x4, matrix products, one_block(): jnp.einsum('qhd,khd->hqk', query_block, key_all, preferred_element_type=j...  10.7 us
  transfers between devices with their start and end apart: 6, of which 6 were waited for; matrix products, arithmetic and copies ran while one was open for 7% of the time, Pallas kernels for 0%

commit v1 on v0

v1 whole, which is shorter than its diff:
```python
import functools
import math

import jax
import jax.numpy as jnp
from jax import lax
from jax.experimental import pallas as pl
from jax.experimental.pallas import tpu as pltpu
from jax.sharding import PartitionSpec as P

MESH = pl.DeviceIdType.MESH
D = 1280
HW = 64
RANK = 16
NREQ = 8
PREFIX = 256
NT = 16
NZ = 8
ROWS = 128
GROUP = 2048
EPS = 1e-06
F32 = jnp.float32
BF16 = jnp.bfloat16
NT_DIMS = (((1,), (1,)), ((), ()))


def place():
    dp = lax.axis_index("dp")
    t = lax.axis_index("tensor")
    return dp, t, t // 2, t % 2


def delta(i):
    half = (i + 1) // 2
    odd = i % 2
    return half * (1 - 2 * odd)


def at_z(z, d):
    return (z + d + NZ) % NZ


class Ring:
    def __init__(self, chunks, zsend, zrecv, psend, precv):
        self.dp, self.t, self.z, self.c = place()
        self.chunks, self.zsend, self.zrecv = chunks, zsend, zrecv
        self.psend, self.precv = psend, precv
        self.started = []
        self.next = (self.dp, at_z(self.z, 1) * 2 + self.c), (self.dp, at_z(self.z, -1) * 2 + self.c)
        self.other = (self.dp, self.z * 2 + (1 - self.c))

    def spot(self, k, block):
        buf, _, r0, n = self.chunks[k]
        return buf.at[block, pl.ds(r0, n)]

    def ring_copy(self, way, step, k, src, block):
        return pltpu.make_async_remote_copy(
            src_ref=src, dst_ref=self.spot(k, block),
            send_sem=self.zsend.at[way, step - 1, k], recv_sem=self.zrecv.at[way, step - 1, k],
            device_id=self.next[way], device_id_type=MESH)

    def core_copy(self, i, k, src, block):
        return pltpu.make_async_remote_copy(
            src_ref=src, dst_ref=self.spot(k, block),
            send_sem=self.psend.at[i, k], recv_sem=self.precv.at[i, k],
            device_id=self.other, device_id_type=MESH)

    def go(self, copy):
        copy.start()
        self.started.append(copy)

    def source(self, k):
        _, src, r0, n = self.chunks[k]
        return src.at[pl.ds(r0, n)]

    def first(self):
        for k in range(len(self.chunks)):
            for way in range(2):
                self.go(self.ring_copy(way, 1, k, self.source(k), self.t))
        for k in range(len(self.chunks)):
            self.go(self.core_copy(0, k, self.source(k), self.t))

    def step(self, s):
        for k in range(len(self.chunks)):
            for way in range(2):
                if s == 4 and k % 2 != way:
                    continue
                block = at_z(self.z, -s if way == 0 else s) * 2 + self.c
                here = self.spot(k, block)
                self.ring_copy(way, s, k, here, block).wait_recv()
                if s < 3 or (s == 3 and k % 2 == way):
                    self.go(self.ring_copy(way, s + 1, k, here, block))
                i = 7 if s == 4 else (2 * s - 1 if way == 0 else 2 * s)
                self.go(self.core_copy(i, k, here, block))

    def from_core(self, i):
        block = at_z(self.z, delta(i)) * 2 + (1 - self.c)
        for k in range(len(self.chunks)):
            self.core_copy(i, k, self.spot(k, block), block).wait_recv()

    def drain(self):
        for copy in self.started:
            copy.wait_send()


class Plane:
    def __init__(self, number, first_axis, src, buf, send, recv, local):
        dp, t, _, _ = place()
        x, y = dp // 4, dp % 4
        self.src, self.buf, self.n, self.send, self.recv, self.local = src, buf, number, send, recv, local
        self.a, self.b = (x, y) if first_axis == 0 else (y, x)

        def device(a, b):
            return (a * 4 + b if first_axis == 0 else b * 4 + a), t

        up_a, down_a = (self.a + 1) % 4, (self.a + 3) % 4
        up_b, down_b = (self.b + 1) % 4, (self.b + 3) % 4
        self.lo_a, self.hi_a, self.lo_b, self.hi_b = down_a, up_a, down_b, up_b
        self.dev_a = device(up_a, self.b), device(down_a, self.b)
        self.dev_b = device(self.a, up_b), device(self.a, down_b)
        self.started = []

    def copy(self, k, src, dst, dev):
        return pltpu.make_async_remote_copy(
            src_ref=src, dst_ref=dst, send_sem=self.send.at[self.n, k], recv_sem=self.recv.at[self.n, k],
            device_id=dev, device_id_type=MESH)

    def go(self, k, src, dst, dev):
        c = self.copy(k, src, dst, dev)
        c.start()
        self.started.append(c)

    def got(self, k, dst):
        self.copy(k, dst, dst, self.dev_a[0]).wait_recv()

    def halves(self, ref):
        n = ref.shape[0] // 2
        return ref.at[pl.ds(0, n)], ref.at[pl.ds(n, n)]

    def one(self):
        mine = self.buf.at[self.b, self.a]
        self.own = pltpu.make_async_copy(self.src, mine, self.local.at[self.n])
        self.own.start()
        self.go(0, self.src, mine, self.dev_a[0])
        self.go(1, self.src, mine, self.dev_a[1])

    def two(self):
        lo, hi = self.buf.at[self.b, self.lo_a], self.buf.at[self.b, self.hi_a]
        self.got(0, lo)
        self.go(2, self.halves(lo)[0], self.halves(lo)[0], self.dev_a[0])
        self.got(1, hi)
        self.go(3, self.halves(hi)[1], self.halves(hi)[1], self.dev_a[1])

    def three(self):
        far = self.buf.at[self.b, (self.a + 2) % 4]
        self.got(2, self.halves(far)[0])
        self.got(3, self.halves(far)[1])
        self.own.wait()
        row = self.buf.at[self.b]
        self.go(4, row, row, self.dev_b[0])
        self.go(5, row, row, self.dev_b[1])

    def four(self):
        lo, hi = self.buf.at[self.lo_b], self.buf.at[self.hi_b]
        self.got(4, lo)
        self.go(6, self.halves(lo)[0], self.halves(lo)[0], self.dev_b[0])
        self.got(5, hi)
        self.go(7, self.halves(hi)[1], self.halves(hi)[1], self.dev_b[1])

    def five(self):
        far = self.buf.at[(self.b + 2) % 4]
        self.got(6, self.halves(far)[0])
        self.got(7, self.halves(far)[1])

    def drain(self):
        for c in self.started:
            c.wait_send()


def greet(peers):
    barrier = pltpu.get_barrier_semaphore()
    for peer in peers:
        pl.semaphore_signal(barrier, inc=1, device_id=peer, device_id_type=MESH)
    pl.semaphore_wait(barrier, len(peers))


def lanes(shape):
    return lax.broadcasted_iota(jnp.int32, shape, len(shape) - 1)


def row_starts(len_ref, first_row, shape):
    rows = first_row + lax.broadcasted_iota(jnp.int32, shape, 0)
    end = jnp.int32(0)
    req = jnp.zeros(shape, jnp.int32)
    start = jnp.zeros(shape, jnp.int32)
    for r in range(NREQ):
        size = len_ref[0, r]
        end = end + size
        past = rows >= end
        req = req + jnp.where(past, 1, 0)
        start = start + jnp.where(past, size, 0)
    return rows, req, start


def gather_kernel(h_ref, o_ref, pg_ref, up_ref, dn_ref, w_ref, gain_ref, len_ref, ra_ref, rp_ref, pt_ref,
                  q_out, kv_out, pkv_out, o_out,
                  gh, go, pb, ub, db, sd, su, trig,
                  zsend, zrecv, psend, precv, xsend, xrecv, local, dsend, drecv):
    dp, t, z, c = place()
    x, y = dp // 4, dp % 4
    greet([
        (dp, at_z(z, 1) * 2 + c), (dp, at_z(z, -1) * 2 + c), (dp, z * 2 + (1 - c)),
        (((x + 1) % 4) * 4 + y, t), (((x + 3) % 4) * 4 + y, t),
        (x * 4 + (y + 1) % 4, t), (x * 4 + (y + 3) % 4, t),
    ])
    ring = Ring([(gh, h_ref, 0, 64), (gh, h_ref, 64, 64), (go, o_ref, 0, 32), (go, o_ref, 32, 32)],
                zsend, zrecv, psend, precv)
    planes = [
        Plane(0, 1, dn_ref.at[pl.ds(2 * c, 2)], db.at[c], xsend, xrecv, local),
        Plane(1, 0, pg_ref, pb, xsend, xrecv, local),
        Plane(2, 1, up_ref, ub, xsend, xrecv, local),
    ]
    for p in planes:
        p.one()
    ring.first()
    own_h = pltpu.make_async_copy(h_ref, gh.at[t], local.at[3])
    own_h.start()
    own_o = pltpu.make_async_copy(o_ref, go.at[t], local.at[4])
    own_o.start()
    for p in planes:
        p.two()
    for p in planes:
        p.three()

    lane = lanes((256, 128))
    frequency = jnp.exp((lane % 32).astype(F32) * (-2.0 * math.log(10000.0) / HW))
    quarter = jnp.where(lane < HW, 0.0, 0.5 * math.pi)

    @pl.loop(0, NZ)
    def _(b):
        rows, _, start = row_starts(len_ref, b * 256, (256, 128))
        angle = (rows - start + PREFIX).astype(F32) * frequency
        trig[b] = jnp.cos(angle - quarter)

    own_h.wait()
    own_o.wait()
    ring.step(1)
    for p in planes:
        p.four()
    ring.step(2)
    for p in planes:
        p.five()
    swap = pltpu.make_async_remote_copy(
        src_ref=db.at[c], dst_ref=db.at[c], send_sem=dsend, recv_sem=drecv,
        device_id=(dp, z * 2 + (1 - c)), device_id_type=MESH)
    swap.start()

    gain = gain_ref[...]
    low = lane < HW

    def unit(v):
        total = jnp.sum(jnp.where(low, v * v, 0.0), axis=1, keepdims=True)
        return v * lax.rsqrt(total + EPS) * gain

    @pl.loop(0, NREQ)
    def _(r):
        prompt = rp_ref[0, r]
        for j in range(4):
            page = pt_ref[prompt, j]
            owner = page // 4
            raw = pb[owner % 4, owner // 4, page % 4].astype(F32)
            low_p = lanes((64, 128)) < HW
            total = jnp.sum(jnp.where(low_p, raw * raw, 0.0), axis=1, keepdims=True)
            unit_key = raw * lax.rsqrt(total + EPS) * gain
            pkv_out[pl.ds(pl.multiple_of(r * PREFIX + j * 64, 64), 64), :] = jnp.where(
                low_p, unit_key, raw).astype(BF16)

    pltpu.make_async_remote_copy(
        src_ref=db.at[1 - c], dst_ref=db.at[1 - c], send_sem=dsend, recv_sem=drecv,
        device_id=(dp, z * 2 + (1 - c)), device_id_type=MESH).wait_recv()
    for r in range(NREQ):
        adapter = ra_ref[0, r]
        owner = adapter // 4
        within = adapter % 4
        sd[r * RANK:(r + 1) * RANK, :] = db[within // 2, owner // 4, owner % 4, within % 2]
        su[r * RANK:(r + 1) * RANK, :] = ub[owner // 4, owner % 4, within]

    def project(i):
        ring.from_core(i)
        zb = at_z(z, delta(i))
        values = gh[pl.ds(zb * 2, 2)].reshape(256, D)
        _, req, _ = row_starts(len_ref, zb * 256, (256, 128))
        middle = lax.dot_general(values, sd[...], NT_DIMS, preferred_element_type=F32)
        middle = jnp.where(lane // RANK == req, middle, 0.0).astype(BF16)
        both = jnp.dot(values, w_ref[...], preferred_element_type=F32) + 0.5 * jnp.dot(
            middle, su[...], preferred_element_type=F32)
        wave = trig[zb]
        cosine = jnp.where(low, wave, 1.0)
        sine = pltpu.roll(wave, HW, 1)
        sine = jnp.where(lane < 32, -sine, jnp.where(low, sine, 0.0))

        def rotate(v):
            other = jnp.where(lane < 32, pltpu.roll(v, 96, 1), pltpu.roll(v, 32, 1))
            return v * cosine + other * sine

        query, key_value = both[:, :128], both[:, 128:]
        rows = pl.ds(pl.multiple_of(zb * 256, 256), 256)
        q_out[rows, :] = unit(rotate(query)).astype(BF16) * jnp.asarray(8.0, BF16)
        kv_out[rows, :] = jnp.where(low, unit(rotate(key_value)), key_value).astype(BF16)

    pl.loop(0, 3)(project)
    ring.step(3)
    pl.loop(3, 5)(project)
    ring.step(4)
    pl.loop(5, 8)(project)
    out = pltpu.make_async_copy(go, o_out, local.at[5])
    out.start()
    ring.drain()
    for p in planes:
        p.drain()
    swap.wait_send()
    out.wait()


def attend_kernel(q_ref, kv_ref, pkv_ref, len_ref, out_ref, acc):
    lane = lanes((256, 128))
    low_key = lanes((256, 128)) < HW

    @pl.loop(0, NZ)
    def _(i):
        first = i * 256
        query = q_ref[pl.ds(pl.multiple_of(first, 256), 256), :]
        rows, _, start = row_starts(len_ref, first, (256, 256))
        end = jnp.int32(0)
        request_lo, request_hi, start_lo = jnp.int32(0), jnp.int32(0), jnp.int32(0)
        for r in range(NREQ):
            size = len_ref[0, r]
            end = end + size
            request_lo = request_lo + jnp.where(first >= end, 1, 0)
            start_lo = start_lo + jnp.where(first >= end, size, 0)
            request_hi = request_hi + jnp.where(first + 255 >= end, 1, 0)
        acc[...] = jnp.zeros_like(acc)

        def add(keys, allowed):
            score = lax.dot_general(query, keys, NT_DIMS, preferred_element_type=F32)
            weight = jnp.where(allowed, jnp.exp(score), 0.0).astype(BF16)
            ones = jnp.where(low_key, jnp.asarray(1.0, BF16), keys)
            acc[...] += jnp.dot(weight, ones, preferred_element_type=F32)

        def prefix(r, begins):
            add(pkv_ref[pl.ds(pl.multiple_of(r * PREFIX, PREFIX), PREFIX), :], start == begins)
            return begins + len_ref[0, r]

        lax.fori_loop(request_lo, request_hi + 1, prefix, start_lo)

        def own(j, carry):
            column = j * 256 + lanes((256, 256))
            add(kv_ref[pl.ds(pl.multiple_of(j * 256, 256), 256), :], (column >= start) & (column <= rows))
            return carry

        lax.fori_loop(start_lo // 256, i + 1, own, 0)
        total = acc[...]
        result = total / pltpu.roll(total, HW, 1)
        for b in range(2):
            top, bottom = result[b * 128:b * 128 + 64], result[b * 128 + 64:b * 128 + 128]
            out_ref[2 * i + b] = jnp.where(lanes((64, 128)) >= HW, top, pltpu.roll(bottom, HW, 1)).astype(BF16)


def renorm(v):
    return v * lax.rsqrt(jnp.mean(v * v, axis=-1, keepdims=True) + EPS)


def mix_kernel(attn_ref, o_ref, h_ref, wu_ref, wg_ref, wd_ref, su_ref, sg_ref, ra_ref, rf_ref, out_ref,
               heads, lhs, om, wu, wg, wd, mixed, part, peer, rr, rl, sr, sl,
               asend, arecv, zsend, zrecv, psend, precv, qsend, qrecv, rsend, rrecv, local):
    dp, t, z, c = place()
    loads = [pltpu.make_async_copy(a, b, local.at[n])
             for n, (a, b) in enumerate([(o_ref, om), (wu_ref, wu), (wg_ref, wg), (wd_ref, wd)])]
    for copy in loads:
        copy.start()
    greet([(dp, (t + n) % NT) for n in range(1, NT)])
    started = []
    order = [8, 9, 7, 10, 6, 11, 5, 12, 4, 13, 3, 14, 2, 15, 1]
    for n in order:
        to = (t + n) % NT
        copy = pltpu.make_async_remote_copy(
            src_ref=attn_ref.at[to], dst_ref=heads.at[t], send_sem=asend.at[n], recv_sem=arecv.at[n],
            device_id=(dp, to), device_id_type=MESH)
        copy.start()
        started.append(copy)
    own = pltpu.make_async_copy(attn_ref.at[t], heads.at[t], local.at[4])
    own.start()
    own.wait()
    for n in order:
        frm = (t + NT - n) % NT
        pltpu.make_async_remote_copy(
            src_ref=attn_ref.at[t], dst_ref=heads.at[frm], send_sem=asend.at[n], recv_sem=arecv.at[n],
            device_id=(dp, frm), device_id_type=MESH).wait_recv()
    high = lanes((64, 128)) >= HW
    for j in range(NT // 2):
        even, odd = heads[2 * j].astype(F32), heads[2 * j + 1].astype(F32)
        cols = slice(128 * j, 128 * j + 128)
        lhs[0:64, cols] = jnp.where(high, odd, pltpu.roll(even, HW, 1)).astype(BF16)
        lhs[64:128, cols] = jnp.where(high, pltpu.roll(odd, HW, 1), even).astype(BF16)
    loads[0].wait()
    attn_sum = jnp.dot(lhs[...], om[...], preferred_element_type=F32)
    base = h_ref[...].astype(F32)
    mine = renorm(base + ra_ref[...] * (renorm(attn_sum) - base)).astype(BF16)
    mixed[t] = mine
    ring = Ring([(mixed, mixed.at[t], 0, 64), (mixed, mixed.at[t], 64, 64)], zsend, zrecv, psend, precv)
    ring.first()
    for copy in loads[1:]:
        copy.wait()

    def swap(i, zb):
        return pltpu.make_async_remote_copy(
            src_ref=part.at[zb * 2 + (1 - c)], dst_ref=peer.at[zb], send_sem=qsend.at[i], recv_sem=qrecv.at[i],
            device_id=(dp, z * 2 + (1 - c)), device_id_type=MESH)

    def feed(i):
        ring.from_core(i)
        zb = at_z(z, delta(i))
        values = mixed[pl.ds(zb * 2, 2)].reshape(256, D)
        up = jnp.dot(values, wu[...], preferred_element_type=F32) * su_ref[...]
        gate = jnp.dot(values, wg[...], preferred_element_type=F32) * sg_ref[...]
        units = (up * (gate / (1.0 + jnp.exp(-gate)))).astype(BF16)
        result = jnp.dot(units, wd[...], preferred_element_type=F32).astype(BF16)
        part[pl.ds(zb * 2, 2)] = result.reshape(2, ROWS, D)
        swap(i, zb).start()

    pl.loop(0, 1)(feed)
    ring.step(1)
    pl.loop(1, 3)(feed)
    ring.step(2)
    pl.loop(3, 5)(feed)
    ring.step(3)
    pl.loop(5, 7)(feed)
    ring.step(4)
    pl.loop(7, 8)(feed)

    def local_sum(zb, k):
        rows = pl.ds(64 * k, 64)
        return part[zb * 2 + c, rows].astype(F32) + peer[zb, rows].astype(F32)

    def rs_copy(way, d, k, src):
        dst = (rr if way == 0 else rl).at[d - 1, pl.ds(64 * k, 64)]
        dev = (dp, at_z(z, 1 if way == 0 else -1) * 2 + c)
        return pltpu.make_async_remote_copy(
            src_ref=src, dst_ref=dst, send_sem=rsend.at[way, d - 1, k], recv_sem=rrecv.at[way, d - 1, k],
            device_id=dev, device_id_type=MESH)

    for d in (4, 3, 2, 1):
        swap(2 * d - 1, at_z(z, -d)).wait_recv()
        if d < 4:
            swap(2 * d, at_z(z, d)).wait_recv()
        for k in range(2):
            for way in range(2):
                if d == 4 and k != way:
                    continue
                rows = pl.ds(64 * k, 64)
                recv, sent = (rr, sr) if way == 0 else (rl, sl)
                value = local_sum(at_z(z, d if way == 0 else -d), k)
                if d < 3 or (d == 3 and k == way):
                    rs_copy(way, d + 1, k, sent.at[d, rows]).wait_recv()
                    value = value + recv[d, rows].astype(F32)
                sent[d - 1, rows] = value.astype(BF16)
                copy = rs_copy(way, d, k, sent.at[d - 1, rows])
                copy.start()
                started.append(copy)
    swap(0, z).wait_recv()
    for k in range(2):
        rows = pl.ds(64 * k, 64)
        value = local_sum(z, k)
        for way in range(2):
            rs_copy(way, 1, k, (sr if way == 0 else sl).at[0, rows]).wait_recv()
        value = value + rr[0, rows].astype(F32) + rl[0, rows].astype(F32)
        base = mixed[t, rows].astype(F32)
        out_ref[rows, :] = renorm(base + rf_ref[...] * (renorm(value) - base)).astype(BF16)
    ring.drain()
    for copy in started:
        copy.wait_send()
    for i in range(NZ):
        swap(i, at_z(z, delta(i))).wait_send()


VM = pl.BlockSpec(memory_space=pltpu.VMEM)
SM = pl.BlockSpec(memory_space=pltpu.SMEM)
HB = pl.BlockSpec(memory_space=pl.ANY)
DMA = pltpu.SemaphoreType.DMA


def local(hidden, lengths, request_prompt, request_adapter, prompt_page_table, prefix_page_cache,
          query_key_value_weight, adapter_down, adapter_up, attention_scale, output_matrix, attention_rate,
          up_matrix, gate_matrix, up_scaling, gate_scaling, down_matrix, feedforward_rate):
    def spread(m):
        return jnp.concatenate([m[..., :HW], jnp.zeros_like(m[..., :HW]), m[..., HW:]], axis=-1)

    weight = spread(query_key_value_weight)
    up = spread(adapter_up)
    down = jnp.swapaxes(adapter_down, 1, 2)
    gain = jnp.concatenate([attention_scale, jnp.ones_like(attention_scale)]).reshape(1, 128)
    queries, key_values, prefix, matrix = pl.pallas_call(
        gather_kernel,
        out_shape=(
            jax.ShapeDtypeStruct((GROUP, 128), BF16),
            jax.ShapeDtypeStruct((GROUP, 128), BF16),
            jax.ShapeDtypeStruct((NREQ * PREFIX, 128), BF16),
            jax.ShapeDtypeStruct((NT, HW, D), BF16),
        ),
        in_specs=[HB, HB, HB, HB, HB, VM, VM, SM, SM, SM, SM],
        out_specs=(VM, VM, VM, HB),
        scratch_shapes=[
            pltpu.VMEM((NT, ROWS, D), BF16),
            pltpu.VMEM((NT, HW, D), BF16),
            pltpu.VMEM((4, 4, 4, 64, 128), BF16),
            pltpu.VMEM((4, 4, 4, RANK, 256), BF16),
            pltpu.VMEM((2, 4, 4, 2, RANK, D), BF16),
            pltpu.VMEM((128, D), BF16),
            pltpu.VMEM((128, 256), BF16),
            pltpu.VMEM((NZ, 256, 128), F32),
            DMA((2, 4, 4)), DMA((2, 4, 4)), DMA((8, 4)), DMA((8, 4)),
            DMA((3, 8)), DMA((3, 8)), DMA((6,)), DMA, DMA,
        ],
        compiler_params=pltpu.CompilerParams(
            collective_id=0, has_side_effects=True, vmem_limit_bytes=60 * 2**20),
        name="gather_project",
    )(hidden, output_matrix, prefix_page_cache, up, down, weight, gain,
      lengths, request_adapter, request_prompt, prompt_page_table)
    attn = pl.pallas_call(
        attend_kernel,
        out_shape=jax.ShapeDtypeStruct((NT, 64, 128), BF16),
        in_specs=[VM, VM, VM, SM],
        out_specs=VM,
        scratch_shapes=[pltpu.VMEM((256, 128), F32)],
        name="attend",
    )(queries, key_values, prefix, lengths)
    return pl.pallas_call(
        mix_kernel,
        out_shape=jax.ShapeDtypeStruct((ROWS, D), BF16),
        in_specs=[VM, HB, VM, HB, HB, HB, VM, VM, VM, VM],
        out_specs=VM,
        scratch_shapes=[
            pltpu.VMEM((NT, 64, 128), BF16),
            pltpu.VMEM((ROWS, NT * HW), BF16),
            pltpu.VMEM((NT * HW, D), BF16),
            pltpu.VMEM((D, 320), BF16),
            pltpu.VMEM((D, 320), BF16),
            pltpu.VMEM((320, D), BF16),
            pltpu.VMEM((NT, ROWS, D), BF16),
            pltpu.VMEM((NT, ROWS, D), BF16),
            pltpu.VMEM((NZ, ROWS, D), BF16),
            pltpu.VMEM((4, ROWS, D), BF16), pltpu.VMEM((4, ROWS, D), BF16),
            pltpu.VMEM((4, ROWS, D), BF16), pltpu.VMEM((4, ROWS, D), BF16),
            DMA((16,)), DMA((16,)), DMA((2, 4, 2)), DMA((2, 4, 2)), DMA((8, 2)), DMA((8, 2)),
            DMA((8,)), DMA((8,)), DMA((2, 4, 2)), DMA((2, 4, 2)), DMA((5,)),
        ],
        compiler_params=pltpu.CompilerParams(
            collective_id=1, has_side_effects=True, vmem_limit_bytes=60 * 2**20),
        name="mix_feed",
    )(attn, matrix.reshape(NT * HW, D), hidden, up_matrix, gate_matrix, down_matrix,
      up_scaling.reshape(1, -1), gate_scaling.reshape(1, -1),
      attention_rate.reshape(1, -1), feedforward_rate.reshape(1, -1))


def solution(mesh):
    placed = (
        P(("dp", "tensor"), None),
        P("dp", None),
        P("dp", None),
        P("dp", None),
        P(),
        P("dp", None, "tensor"),
        P(None, "tensor"),
        P("dp", None, None),
        P("dp", None, "tensor"),
        P("tensor"),
        P("tensor", None),
        P(),
        P(None, "tensor"),
        P(None, "tensor"),
        P("tensor"),
        P("tensor"),
        P("tensor", None),
        P(),
    )
    return jax.shard_map(
        local, mesh=mesh, in_specs=placed, out_specs=P(("dp", "tensor"), None), check_vma=False
    )
```

time: 399 us -> 160 us (0.40)
  waiting for transfers between devices: 266 us -> 0 us
  Pallas kernels: 0 us -> 148 us
  matrix products: 51.4 us -> 0 us
  blocking collectives: 20.5 us -> 0 us
  local copies, waits for them, and re-layouts: 25.6 us -> 9.55 us
  between operations: 13.9 us -> 0.1 us
  other arithmetic: 15.1 us -> 1.61 us
    pallas_call x0 -> x3, Pallas kernels: none -> 148 us  [the longest x1 74.2 us: local(): pl.pallas_call(mix_kernel, out_shape=jax.ShapeDtypeStruct((ROWS, D), BF16...]
    all_gather x4 -> x0, waiting for transfers between devices: 145 us -> none  [the longest x1 50 us: local(): lax.all_gather(adapter_down, 'dp', axis=0, tiled=True)]
    reduce_scatter x2 -> x0, waiting for transfers between devices: 120 us -> none  [the longest x1 59.8 us: local(): lax.psum_scatter(jnp.dot(unit_values, down_matrix, preferred_element_type...]
    dot_general x15 -> x0, matrix products: 51.4 us -> none  [the longest x4 10.7 us: one_block(): jnp.einsum('qhd,khd->hqk', query_block, key_all, preferred_element_type=j...]
    all_gather x1 -> x0, blocking collectives: 20.5 us -> none  [local(): lax.all_gather(adapter_up, 'dp', axis=0, tiled=True)]
    all_gather x1 -> x0, local copies, waits for them, and re-layouts: 9.7 us -> none  [local(): lax.all_gather(adapter_down, 'dp', axis=0, tiled=True)]
    reduce_sum x8 -> x0, other arithmetic: 5.75 us -> none  [the longest x4 4.86 us: renorm(): jnp.mean(matrix * matrix, axis=-1, keepdims=True) + epsilon]
    convert_element_type x4 -> x0, other arithmetic: 5.35 us -> none  [the longest x1 2.08 us: local(): renorm(base_rows + attention_rate * (renorm(attn_sum) - base_rows))]
  transfers between devices with their start and end apart: 6 -> 0, of which waited for: 6 -> 0; matrix products, arithmetic and copies ran while one was open for 7% -> 0% of each run, Pallas kernels for 0% -> 0%
where the time goes in v1:
time: 160 us; the launch traced here: 159 us
  Pallas kernels  148 us (92%)
  local copies, waits for them, and re-layouts  9.55 us (6%)
  other arithmetic  1.61 us (1%)
    pallas_call x1, Pallas kernels, local(): pl.pallas_call(mix_kernel, out_shape=jax.ShapeDtypeStruct((ROWS, D), BF16...  74.2 us
    pallas_call x1, Pallas kernels, local(): pl.pallas_call(gather_kernel, out_shape=(jax.ShapeDtypeStruct((GROUP, 128...  56.8 us
    pallas_call x1, Pallas kernels, local(): pl.pallas_call(attend_kernel, out_shape=jax.ShapeDtypeStruct((NT, 64, 128...  16.8 us
    unnamed x24, local copies, waits for them, and re-layouts  5.49 us

profile of v1, /device:TPU:1, one launch (start us, length us, event | category | flops | bytes accessed | tf_op | source)
XLA Modules:
  0.0 159.1 jit_solution(9230589308322927631)
XLA Ops:
  0.0 0.0 slice-start
  0.0 0.1 pad.5.clone
  0.1 1.0 slice.15
  1.1 0.0 copy-start.2
  1.1 0.0 slice-start.1
  1.1 0.0 copy-start.5
  1.1 0.0 copy-start.8
  1.1 0.2 copy.25
  1.3 0.0 slice-done
  1.3 0.2 copy.24
  1.6 1.0 pad_maximum_fusion.w_ref
  2.6 0.0 copy-done.2
  2.6 0.1 slice.13
  2.6 0.0 slice-done.1
  2.6 0.6 pad_maximum_fusion.1.up_ref
  3.3 0.0 copy-done.5
  3.3 0.7 copy.21.pt_ref
  4.0 0.0 copy-done.8
  4.0 0.5 pad_bitcast_fusion.gain_ref
  4.5 0.0 copy-start
  4.5 56.8 %gather_project.1 = (bf16[2048,128]{1,0:T(8,128)(2,1)}, bf16[2048,128]{1,0:T(8,128)(2,1)}, bf16[2048,128]{1,0:T(8,128)(2,1)}, bf16[16,64,1280]{2,1,0:T(8,128)(2,1)}) custom-call(bf16[128,1280]{1,0:T(8,128)(2,1)} %h_ref.3, bf16[64,1280]{1,0:T(8,128)(2,1)} %o_ref.1, bf16[4,64,128]{2,1,0:T(8,128)(2,1)} %pg_ref.1, bf16[4,16,256]{2,1,0:T(8,128)(2,1)} %pad_maximum_fusion.1.up_ref, ...), custom_call_target="tpu_custom_call" | custom-call | tf_op jit(solution)/shard_map/gather_project/pallas_call | solution.py:502
  61.3 16.8 %attend.1.attn_ref = bf16[16,64,128]{2,1,0:T(8,128)(2,1)} custom-call(bf16[2048,128]{1,0:T(8,128)(2,1)} %get-tuple-element.9.q_ref, bf16[2048,128]{1,0:T(8,128)(2,1)} %get-tuple-element.10.kv_ref, bf16[2048,128]{1,0:T(8,128)(2,1)} %get-tuple-element.11.pkv_ref, s32[1,8]{1,0:T(1,128)} %len_ref.3), custom_call_target="tpu_custom_call" | custom-call | tf_op jit(solution)/shard_map/attend/pallas_call | solution.py:529
  78.1 0.0 copy-start.1
  78.1 0.0 copy-done
  78.1 1.3 copy.22.wu_ref
  79.4 0.0 copy-done.1
  79.4 0.0 copy-start.3
  79.4 0.0 copy-start.4
  79.4 0.0 copy-start.6
  79.4 0.0 copy-start.7
  79.4 1.3 copy.23.wg_ref
  80.8 0.0 copy-done.3
  80.8 0.6 reshape.22.ra_ref
  81.4 0.0 copy-done.4
  81.4 0.6 reshape.23.rf_ref
  82.0 0.0 copy-done.6
  82.0 0.6 reshape.20.su_ref
  82.6 0.0 copy-done.7
  82.6 0.6 reshape.21.sg_ref
  83.1 74.2 %mix_feed.1 = bf16[128,1280]{1,0:T(8,128)(2,1)} custom-call(bf16[16,64,128]{2,1,0:T(8,128)(2,1)} %attend.1.attn_ref, bf16[1024,1280]{1,0:T(8,128)(2,1)} %bitcast.4, bf16[128,1280]{1,0:T(8,128)(2,1)} %h_ref.3, bf16[1280,320]{1,0:T(8,128)(2,1)} %copy.22.wu_ref, bf16[1280,320]{1,0:T(8,128)(2,1)} %copy.23.wg_ref, bf16[320,1280]{1,0:T(8,128)(2,1)} %wd_ref.1, ...), custom_call_target="tpu_custom_call" | custom-call | tf_op jit(solution)/shard_map/mix_feed/pallas_call | solution.py:537
  157.3 1.7 %copy.27 = bf16[128,1280]{1,0:T(8,128)(2,1)} copy(bf16[128,1280]{1,0:T(8,128)(2,1)} %mix_feed.1) | data formatting | bytes 655360
  (1 shorter events, 0.0 us)
Async XLA Ops:
  0.0 1.3 slice-start
  1.1 1.5 copy-start.2
  1.1 1.5 slice-start.1
  1.1 2.2 %copy-start.5 = (s32[32,4]{0,1:T(4,128)S(1)}, s32[32,4]{0,1:T(4,128)}, u32[]{:S(2)}) copy-start(s32[32,4]{0,1:T(4,128)} %param.22) | copy-start | bytes 1540
  1.1 2.8 %copy-start.8 = (f32[64]{0:T(128)S(1)}, f32[64]{0:T(128)}, u32[]{:S(2)}) copy-start(f32[64]{0:T(128)} %param.27) | copy-start | bytes 772
  4.5 73.6 %copy-start = (bf16[1280,320]{0,1:T(8,128)(2,1)S(1)}, bf16[1280,320]{0,1:T(8,128)(2,1)}, u32[]{:S(2)}) copy-start(bf16[1280,320]{0,1:T(8,128)(2,1)} %param.30) | copy-start | bytes 2457604
  78.1 1.3 copy-start.1
  79.4 1.3 copy-start.3
  79.4 1.9 %copy-start.4 = (f32[1280]{0:T(1024)S(1)}, f32[1280]{0:T(1024)}, u32[]{:S(2)}) copy-start(f32[1280]{0:T(1024)} %param.35) | copy-start | bytes 15364
  79.4 2.5 %copy-start.6 = (f32[320]{0:T(512)S(1)}, f32[320]{0:T(512)}, u32[]{:S(2)}) copy-start(f32[320]{0:T(512)} %param.32) | copy-start | bytes 3844
  79.4 3.1 %copy-start.7 = (f32[320]{0:T(512)S(1)}, f32[320]{0:T(512)}, u32[]{:S(2)}) copy-start(f32[320]{0:T(512)} %param.33) | copy-start | bytes 3844

commit v2 on v1

--- a/solution.py
+++ b/solution.py
@@ -74,21 +74,26 @@
         return src.at[pl.ds(r0, n)]
 
     def first(self):
-        for k in range(len(self.chunks)):
+        for ks in self.order():
             for way in range(2):
-                self.go(self.ring_copy(way, 1, k, self.source(k), self.t))
+                self.go(self.ring_copy(way, 1, ks[way], self.source(ks[way]), self.t))
         for k in range(len(self.chunks)):
             self.go(self.core_copy(0, k, self.source(k), self.t))
 
+    def order(self):
+        n = len(self.chunks)
+        return [(k, (k + n // 2) % n) for k in range(n)]
+
     def step(self, s):
-        for k in range(len(self.chunks)):
+        for n, ks in enumerate(self.order()):
             for way in range(2):
-                if s == 4 and k % 2 != way:
+                k, far = ks[way], n < len(self.chunks) // 2
+                if s == 4 and not far:
                     continue
                 block = at_z(self.z, -s if way == 0 else s) * 2 + self.c
                 here = self.spot(k, block)
                 self.ring_copy(way, s, k, here, block).wait_recv()
-                if s < 3 or (s == 3 and k % 2 == way):
+                if s < 3 or (s == 3 and far):
                     self.go(self.ring_copy(way, s + 1, k, here, block))
                 i = 7 if s == 4 else (2 * s - 1 if way == 0 else 2 * s)
                 self.go(self.core_copy(i, k, here, block))
@@ -134,6 +139,9 @@
         self.copy(k, dst, dst, self.dev_a[0]).wait_recv()
 
     def halves(self, ref):
+        if len(ref.shape) == 2:
+            n = ref.shape[1] // 2
+            return ref.at[:, pl.ds(0, n)], ref.at[:, pl.ds(n, n)]
         n = ref.shape[0] // 2
         return ref.at[pl.ds(0, n)], ref.at[pl.ds(n, n)]
 
@@ -203,8 +211,8 @@
 
 
 def gather_kernel(h_ref, o_ref, pg_ref, up_ref, dn_ref, w_ref, gain_ref, len_ref, ra_ref, rp_ref, pt_ref,
-                  q_out, kv_out, pkv_out, o_out,
-                  gh, go, pb, ub, db, sd, su, trig,
+                  q_out, kv_out, o_out,
+                  gh, go, pb, ub, db, wide, sel, tail, su, gains, trig,
                   zsend, zrecv, psend, precv, xsend, xrecv, local, dsend, drecv):
     dp, t, z, c = place()
     x, y = dp // 4, dp % 4
@@ -213,19 +221,20 @@
         (((x + 1) % 4) * 4 + y, t), (((x + 3) % 4) * 4 + y, t),
         (x * 4 + (y + 1) % 4, t), (x * 4 + (y + 3) % 4, t),
     ])
-    ring = Ring([(gh, h_ref, 0, 64), (gh, h_ref, 64, 64), (go, o_ref, 0, 32), (go, o_ref, 32, 32)],
+    ring = Ring([(gh, h_ref, 0, 64), (go, o_ref, 0, 32), (gh, h_ref, 64, 64), (go, o_ref, 32, 32)],
                 zsend, zrecv, psend, precv)
-    planes = [
-        Plane(0, 1, dn_ref.at[pl.ds(2 * c, 2)], db.at[c], xsend, xrecv, local),
-        Plane(1, 0, pg_ref, pb, xsend, xrecv, local),
-        Plane(2, 1, up_ref, ub, xsend, xrecv, local),
-    ]
+    planes = []
+    for half in range(2):
+        for src, buf in ((dn_ref.at[2 * c + half], db.at[c, half]),
+                         (pg_ref.at[pl.ds(2 * half, 2)], pb.at[half]),
+                         (up_ref.at[pl.ds(2 * half, 2)], ub.at[half])):
+            planes.append(Plane(len(planes), half, src, buf, xsend, xrecv, local))
+    ring.first()
     for p in planes:
         p.one()
-    ring.first()
-    own_h = pltpu.make_async_copy(h_ref, gh.at[t], local.at[3])
+    own_h = pltpu.make_async_copy(h_ref, gh.at[t], local.at[6])
     own_h.start()
-    own_o = pltpu.make_async_copy(o_ref, go.at[t], local.at[4])
+    own_o = pltpu.make_async_copy(o_ref, go.at[t], local.at[7])
     own_o.start()
     for p in planes:
         p.two()
@@ -233,8 +242,16 @@
         p.three()
 
     lane = lanes((256, 128))
+    low = lane < HW
+    gains[...] = jnp.ones_like(gains)
+    gains[:, 0:HW] = jnp.broadcast_to(gain_ref[...].reshape(1, HW), (8, HW))
+    gain = gains[0:1, :]
+    wide[128:192, :] = w_ref[0:HW, :]
+    wide[192:256, :] = jnp.zeros((HW, D), BF16)
+    wide[256:384, :] = w_ref[HW:3 * HW, :]
+    tail[...] = jnp.zeros_like(tail)
     frequency = jnp.exp((lane % 32).astype(F32) * (-2.0 * math.log(10000.0) / HW))
-    quarter = jnp.where(lane < HW, 0.0, 0.5 * math.pi)
+    quarter = jnp.where(low, 0.0, 0.5 * math.pi)
 
     @pl.loop(0, NZ)
     def _(b):
@@ -250,50 +267,62 @@
     ring.step(2)
     for p in planes:
         p.five()
-    swap = pltpu.make_async_remote_copy(
-        src_ref=db.at[c], dst_ref=db.at[c], send_sem=dsend, recv_sem=drecv,
-        device_id=(dp, z * 2 + (1 - c)), device_id_type=MESH)
-    swap.start()
-
-    gain = gain_ref[...]
-    low = lane < HW
+    swaps = []
+    for half in range(2):
+        swap = pltpu.make_async_remote_copy(
+            src_ref=db.at[c, half], dst_ref=db.at[c, half], send_sem=dsend.at[half], recv_sem=drecv.at[half],
+            device_id=(dp, z * 2 + (1 - c)), device_id_type=MESH)
+        swap.start()
+        swaps.append(swap)
 
     def unit(v):
         total = jnp.sum(jnp.where(low, v * v, 0.0), axis=1, keepdims=True)
         return v * lax.rsqrt(total + EPS) * gain
+
+    def slot(owner, half):
+        a, b = owner // 4, owner % 4
+        return b + half * (a - b), a + half * (b - a)
 
     @pl.loop(0, NREQ)
     def _(r):
         prompt = rp_ref[0, r]
         for j in range(4):
-            page = pt_ref[prompt, j]
-            owner = page // 4
-            raw = pb[owner % 4, owner // 4, page % 4].astype(F32)
+            page = pt_ref[j, prompt]
+            half = (page % 4) // 2
+            major, minor = slot(page // 4, half)
+            raw = pb[half, major, minor, page % 2].astype(F32)
             low_p = lanes((64, 128)) < HW
             total = jnp.sum(jnp.where(low_p, raw * raw, 0.0), axis=1, keepdims=True)
             unit_key = raw * lax.rsqrt(total + EPS) * gain
-            pkv_out[pl.ds(pl.multiple_of(r * PREFIX + j * 64, 64), 64), :] = jnp.where(
+            kv_out[pl.ds(pl.multiple_of(r * PREFIX + j * 64, 64), 64), :] = jnp.where(
                 low_p, unit_key, raw).astype(BF16)
 
-    pltpu.make_async_remote_copy(
-        src_ref=db.at[1 - c], dst_ref=db.at[1 - c], send_sem=dsend, recv_sem=drecv,
-        device_id=(dp, z * 2 + (1 - c)), device_id_type=MESH).wait_recv()
+    for half in range(2):
+        pltpu.make_async_remote_copy(
+            src_ref=db.at[1 - c, half], dst_ref=db.at[1 - c, half],
+            send_sem=dsend.at[half], recv_sem=drecv.at[half],
+            device_id=(dp, z * 2 + (1 - c)), device_id_type=MESH).wait_recv()
     for r in range(NREQ):
         adapter = ra_ref[0, r]
-        owner = adapter // 4
         within = adapter % 4
-        sd[r * RANK:(r + 1) * RANK, :] = db[within // 2, owner // 4, owner % 4, within % 2]
-        su[r * RANK:(r + 1) * RANK, :] = ub[owner // 4, owner % 4, within]
+        major, minor = slot(adapter // 4, within % 2)
+        wide[r * RANK:(r + 1) * RANK, :] = db[within // 2, within % 2, major, minor]
+        major, minor = slot(adapter // 4, within // 2)
+        sel[r * RANK:(r + 1) * RANK, :] = ub[within // 2, major, minor, within % 2].astype(F32)
+    first = sel[:, 0:128]
+    tail[:, 0:HW] = sel[:, 128:192]
+    low_s = lanes((128, 128)) < HW
+    su[:, 0:128] = jnp.where(low_s, first, 0.0).astype(BF16)
+    su[:, 128:256] = jnp.where(low_s, pltpu.roll(first, HW, 1), pltpu.roll(tail[...], HW, 1)).astype(BF16)
 
     def project(i):
         ring.from_core(i)
         zb = at_z(z, delta(i))
         values = gh[pl.ds(zb * 2, 2)].reshape(256, D)
         _, req, _ = row_starts(len_ref, zb * 256, (256, 128))
-        middle = lax.dot_general(values, sd[...], NT_DIMS, preferred_element_type=F32)
-        middle = jnp.where(lane // RANK == req, middle, 0.0).astype(BF16)
-        both = jnp.dot(values, w_ref[...], preferred_element_type=F32) + 0.5 * jnp.dot(
-            middle, su[...], preferred_element_type=F32)
+        every = lax.dot_general(values, wide[...], NT_DIMS, preferred_element_type=F32)
+        middle = jnp.where(lane // RANK == req, every[:, 0:128], 0.0).astype(BF16)
+        both = every[:, 128:384] + 0.5 * jnp.dot(middle, su[...], preferred_element_type=F32)
         wave = trig[zb]
         cosine = jnp.where(low, wave, 1.0)
         sine = pltpu.roll(wave, HW, 1)
@@ -304,27 +333,37 @@
             return v * cosine + other * sine
 
         query, key_value = both[:, :128], both[:, 128:]
-        rows = pl.ds(pl.multiple_of(zb * 256, 256), 256)
-        q_out[rows, :] = unit(rotate(query)).astype(BF16) * jnp.asarray(8.0, BF16)
-        kv_out[rows, :] = jnp.where(low, unit(rotate(key_value)), key_value).astype(BF16)
+        row = pl.multiple_of(zb * 256, 256)
+        q_out[pl.ds(row, 256), :] = unit(rotate(query)).astype(BF16) * jnp.asarray(8.0, BF16)
+        kv_out[pl.ds(row + NREQ * PREFIX, 256), :] = jnp.where(
+            low, unit(rotate(key_value)), key_value).astype(BF16)
 
     pl.loop(0, 3)(project)
     ring.step(3)
     pl.loop(3, 5)(project)
     ring.step(4)
     pl.loop(5, 8)(project)
-    out = pltpu.make_async_copy(go, o_out, local.at[5])
+    out = pltpu.make_async_copy(go, o_out, local.at[8])
     out.start()
     ring.drain()
     for p in planes:
         p.drain()
-    swap.wait_send()
+    for swap in swaps:
+        swap.wait_send()
     out.wait()
 
 
-def attend_kernel(q_ref, kv_ref, pkv_ref, len_ref, out_ref, acc):
-    lane = lanes((256, 128))
-    low_key = lanes((256, 128)) < HW
+TILES = 2
+
+
+def attend_kernel(q_ref, kv_ref, len_ref, out_ref, acc, begins):
+    low = lanes((256, 128)) < HW
+    begin = jnp.int32(0)
+    for r in range(NREQ):
+        begins[r] = begin
+        begin = begin + len_ref[0, r]
+    for r in range(NREQ, 2 * NREQ):
+        begins[r] = jnp.int32(0)
 
     @pl.loop(0, NZ)
     def _(i):
@@ -340,25 +379,29 @@
             start_lo = start_lo + jnp.where(first >= end, size, 0)
             request_hi = request_hi + jnp.where(first + 255 >= end, 1, 0)
         acc[...] = jnp.zeros_like(acc)
-
-        def add(keys, allowed):
-            score = lax.dot_general(query, keys, NT_DIMS, preferred_element_type=F32)
-            weight = jnp.where(allowed, jnp.exp(score), 0.0).astype(BF16)
-            ones = jnp.where(low_key, jnp.asarray(1.0, BF16), keys)
-            acc[...] += jnp.dot(weight, ones, preferred_element_type=F32)
-
-        def prefix(r, begins):
-            add(pkv_ref[pl.ds(pl.multiple_of(r * PREFIX, PREFIX), PREFIX), :], start == begins)
-            return begins + len_ref[0, r]
-
-        lax.fori_loop(request_lo, request_hi + 1, prefix, start_lo)
-
-        def own(j, carry):
-            column = j * 256 + lanes((256, 256))
-            add(kv_ref[pl.ds(pl.multiple_of(j * 256, 256), 256), :], (column >= start) & (column <= rows))
-            return carry
-
-        lax.fori_loop(start_lo // 256, i + 1, own, 0)
+        lowest = start_lo // 256
+        prefixes = request_hi + 1 - request_lo
+        count = prefixes + i + 1 - lowest
+        lane = lanes((256, 256))
+
+        @pl.loop(0, (count + TILES - 1) // TILES)
+        def _(n):
+            total = None
+            for u in range(TILES):
+                m = jnp.minimum(n * TILES + u, count - 1)
+                shared = m < prefixes
+                tile = jnp.where(shared, request_lo + m, NREQ + lowest + m - prefixes)
+                base = jnp.where(shared, begins[tile], (tile - NREQ) * 256)
+                base = jnp.where(n * TILES + u < count, base, 2 * GROUP)
+                column = jnp.where(shared, 0, 1) * lane + base
+                keys = kv_ref[pl.ds(pl.multiple_of(tile * 256, 256), 256), :]
+                score = lax.dot_general(query, keys, NT_DIMS, preferred_element_type=F32)
+                weight = jnp.where((column >= start) & (column <= rows), jnp.exp(score), 0.0).astype(BF16)
+                ones = jnp.where(low, jnp.asarray(1.0, BF16), keys)
+                part = jnp.dot(weight, ones, preferred_element_type=F32)
+                total = part if total is None else total + part
+            acc[...] += total
+
         total = acc[...]
         result = total / pltpu.roll(total, HW, 1)
         for b in range(2):
@@ -370,14 +413,10 @@
     return v * lax.rsqrt(jnp.mean(v * v, axis=-1, keepdims=True) + EPS)
 
 
-def mix_kernel(attn_ref, o_ref, h_ref, wu_ref, wg_ref, wd_ref, su_ref, sg_ref, ra_ref, rf_ref, out_ref,
+def mix_kernel(attn_ref, o_ref, h_ref, wu_ref, wg_ref, wd_ref, su_ref, sg_ref, ra_ref, sum_out, mixed_out,
                heads, lhs, om, wu, wg, wd, mixed, part, peer, rr, rl, sr, sl,
                asend, arecv, zsend, zrecv, psend, precv, qsend, qrecv, rsend, rrecv, local):
     dp, t, z, c = place()
-    loads = [pltpu.make_async_copy(a, b, local.at[n])
-             for n, (a, b) in enumerate([(o_ref, om), (wu_ref, wu), (wg_ref, wg), (wd_ref, wd)])]
-    for copy in loads:
-        copy.start()
     greet([(dp, (t + n) % NT) for n in range(1, NT)])
     started = []
     order = [8, 9, 7, 10, 6, 11, 5, 12, 4, 13, 3, 14, 2, 15, 1]
@@ -390,6 +429,11 @@
         started.append(copy)
     own = pltpu.make_async_copy(attn_ref.at[t], heads.at[t], local.at[4])
     own.start()
+    loads = [pltpu.make_async_copy(a, b, local.at[n])
+             for n, (a, b) in enumerate([(o_ref, om), (wu_ref, wu), (wg_ref, wg), (wd_ref, wd)])]
+    for copy in loads:
+        copy.start()
+    base = h_ref[...].astype(F32)
     own.wait()
     for n in order:
         frm = (t + NT - n) % NT
@@ -404,13 +448,15 @@
         lhs[64:128, cols] = jnp.where(high, pltpu.roll(odd, HW, 1), even).astype(BF16)
     loads[0].wait()
     attn_sum = jnp.dot(lhs[...], om[...], preferred_element_type=F32)
-    base = h_ref[...].astype(F32)
-    mine = renorm(base + ra_ref[...] * (renorm(attn_sum) - base)).astype(BF16)
+    rate = ra_ref[...].reshape(1, D)
+    mine = renorm(base + rate * (renorm(attn_sum) - base)).astype(BF16)
     mixed[t] = mine
-    ring = Ring([(mixed, mixed.at[t], 0, 64), (mixed, mixed.at[t], 64, 64)], zsend, zrecv, psend, precv)
+    ring = Ring([(mixed, mixed.at[t], 32 * k, 32) for k in range(4)], zsend, zrecv, psend, precv)
     ring.first()
+    mixed_out[...] = mine
     for copy in loads[1:]:
         copy.wait()
+    scale_up, scale_gate = su_ref[...].reshape(1, 320), sg_ref[...].reshape(1, 320)
 
     def swap(i, zb):
         return pltpu.make_async_remote_copy(
@@ -421,12 +467,43 @@
         ring.from_core(i)
         zb = at_z(z, delta(i))
         values = mixed[pl.ds(zb * 2, 2)].reshape(256, D)
-        up = jnp.dot(values, wu[...], preferred_element_type=F32) * su_ref[...]
-        gate = jnp.dot(values, wg[...], preferred_element_type=F32) * sg_ref[...]
+        up = lax.dot_general(values, wu[...], NT_DIMS, preferred_element_type=F32) * scale_up
+        gate = lax.dot_general(values, wg[...], NT_DIMS, preferred_element_type=F32) * scale_gate
         units = (up * (gate / (1.0 + jnp.exp(-gate)))).astype(BF16)
         result = jnp.dot(units, wd[...], preferred_element_type=F32).astype(BF16)
         part[pl.ds(zb * 2, 2)] = result.reshape(2, ROWS, D)
         swap(i, zb).start()
+
+    def local_sum(zb, k):
+        rows = pl.ds(32 * k, 32)
+        return part[zb * 2 + c, rows].astype(F32) + peer[zb, rows].astype(F32)
+
+    def rs_copy(way, d, k, src):
+        dst = (rr if way == 0 else rl).at[d - 1, pl.ds(32 * k, 32)]
+        dev = (dp, at_z(z, 1 if way == 0 else -1) * 2 + c)
+        return pltpu.make_async_remote_copy(
+            src_ref=src, dst_ref=dst, send_sem=rsend.at[way, d - 1, k], recv_sem=rrecv.at[way, d - 1, k],
+            device_id=dev, device_id_type=MESH)
+
+    def pass_on(d, near, far):
+        for n in ([2, 3] if near else []) + ([0, 1] if far else []):
+            for way in range(2):
+                k = (n + 2 * way) % 4
+                rows = pl.ds(32 * k, 32)
+                recv, sent = (rr, sr) if way == 0 else (rl, sl)
+                value = local_sum(at_z(z, d if way == 0 else -d), k)
+                if d < 3 or (d == 3 and n < 2):
+                    rs_copy(way, d + 1, k, sent.at[d, rows]).wait_recv()
+                    value = value + recv[d, rows].astype(F32)
+                sent[d - 1, rows] = value.astype(BF16)
+                copy = rs_copy(way, d, k, sent.at[d - 1, rows])
+                copy.start()
+                started.append(copy)
+
+    def swapped(d):
+        swap(2 * d - 1, at_z(z, -d)).wait_recv()
+        if d < 4:
+            swap(2 * d, at_z(z, d)).wait_recv()
 
     pl.loop(0, 1)(feed)
     ring.step(1)
@@ -435,47 +512,24 @@
     pl.loop(3, 5)(feed)
     ring.step(3)
     pl.loop(5, 7)(feed)
+    swapped(3)
+    pass_on(3, True, False)
     ring.step(4)
     pl.loop(7, 8)(feed)
-
-    def local_sum(zb, k):
-        rows = pl.ds(64 * k, 64)
-        return part[zb * 2 + c, rows].astype(F32) + peer[zb, rows].astype(F32)
-
-    def rs_copy(way, d, k, src):
-        dst = (rr if way == 0 else rl).at[d - 1, pl.ds(64 * k, 64)]
-        dev = (dp, at_z(z, 1 if way == 0 else -1) * 2 + c)
-        return pltpu.make_async_remote_copy(
-            src_ref=src, dst_ref=dst, send_sem=rsend.at[way, d - 1, k], recv_sem=rrecv.at[way, d - 1, k],
-            device_id=dev, device_id_type=MESH)
-
-    for d in (4, 3, 2, 1):
-        swap(2 * d - 1, at_z(z, -d)).wait_recv()
-        if d < 4:
-            swap(2 * d, at_z(z, d)).wait_recv()
-        for k in range(2):
-            for way in range(2):
-                if d == 4 and k != way:
-                    continue
-                rows = pl.ds(64 * k, 64)
-                recv, sent = (rr, sr) if way == 0 else (rl, sl)
-                value = local_sum(at_z(z, d if way == 0 else -d), k)
-                if d < 3 or (d == 3 and k == way):
-                    rs_copy(way, d + 1, k, sent.at[d, rows]).wait_recv()
-                    value = value + recv[d, rows].astype(F32)
-                sent[d - 1, rows] = value.astype(BF16)
-                copy = rs_copy(way, d, k, sent.at[d - 1, rows])
-                copy.start()
-                started.append(copy)
+    swapped(4)
+    pass_on(4, False, True)
+    pass_on(3, False, True)
+    swapped(2)
+    pass_on(2, True, True)
+    swapped(1)
+    pass_on(1, True, True)
     swap(0, z).wait_recv()
-    for k in range(2):
-        rows = pl.ds(64 * k, 64)
+    for k in range(4):
+        rows = pl.ds(32 * k, 32)
         value = local_sum(z, k)
         for way in range(2):
             rs_copy(way, 1, k, (sr if way == 0 else sl).at[0, rows]).wait_recv()
-        value = value + rr[0, rows].astype(F32) + rl[0, rows].astype(F32)
-        base = mixed[t, rows].astype(F32)
-        out_ref[rows, :] = renorm(base + rf_ref[...] * (renorm(value) - base)).astype(BF16)
+        sum_out[rows, :] = value + rr[0, rows].astype(F32) + rl[0, rows].astype(F32)
     ring.drain()
     for copy in started:
         copy.wait_send()
@@ -483,6 +537,12 @@
         swap(i, at_z(z, delta(i))).wait_send()
 
 
+def finish_kernel(sum_ref, mixed_ref, rate_ref, out_ref):
+    base = mixed_ref[...].astype(F32)
+    rate = rate_ref[...].reshape(1, D)
+    out_ref[...] = renorm(base + rate * (renorm(sum_ref[...]) - base)).astype(BF16)
+
+
 VM = pl.BlockSpec(memory_space=pltpu.VMEM)
 SM = pl.BlockSpec(memory_space=pltpu.SMEM)
 HB = pl.BlockSpec(memory_space=pl.ANY)
@@ -492,74 +552,76 @@
 def local(hidden, lengths, request_prompt, request_adapter, prompt_page_table, prefix_page_cache,
           query_key_value_weight, adapter_down, adapter_up, attention_scale, output_matrix, attention_rate,
           up_matrix, gate_matrix, up_scaling, gate_scaling, down_matrix, feedforward_rate):
-    def spread(m):
-        return jnp.concatenate([m[..., :HW], jnp.zeros_like(m[..., :HW]), m[..., HW:]], axis=-1)
-
-    weight = spread(query_key_value_weight)
-    up = spread(adapter_up)
-    down = jnp.swapaxes(adapter_down, 1, 2)
-    gain = jnp.concatenate([attention_scale, jnp.ones_like(attention_scale)]).reshape(1, 128)
-    queries, key_values, prefix, matrix = pl.pallas_call(
+    queries, key_values, matrix = pl.pallas_call(
         gather_kernel,
         out_shape=(
             jax.ShapeDtypeStruct((GROUP, 128), BF16),
-            jax.ShapeDtypeStruct((GROUP, 128), BF16),
-            jax.ShapeDtypeStruct((NREQ * PREFIX, 128), BF16),
+            jax.ShapeDtypeStruct((NREQ * PREFIX + GROUP, 128), BF16),
             jax.ShapeDtypeStruct((NT, HW, D), BF16),
         ),
         in_specs=[HB, HB, HB, HB, HB, VM, VM, SM, SM, SM, SM],
-        out_specs=(VM, VM, VM, HB),
+        out_specs=(VM, VM, HB),
         scratch_shapes=[
             pltpu.VMEM((NT, ROWS, D), BF16),
             pltpu.VMEM((NT, HW, D), BF16),
-            pltpu.VMEM((4, 4, 4, 64, 128), BF16),
-            pltpu.VMEM((4, 4, 4, RANK, 256), BF16),
-            pltpu.VMEM((2, 4, 4, 2, RANK, D), BF16),
-            pltpu.VMEM((128, D), BF16),
+            pltpu.VMEM((2, 4, 4, 2, 64, 128), BF16),
+            pltpu.VMEM((2, 4, 4, 2, RANK, 192), BF16),
+            pltpu.VMEM((2, 2, 4, 4, RANK, D), BF16),
+            pltpu.VMEM((384, D), BF16),
+            pltpu.VMEM((128, 192), F32),
+            pltpu.VMEM((128, 128), F32),
             pltpu.VMEM((128, 256), BF16),
+            pltpu.VMEM((8, 128), F32),
             pltpu.VMEM((NZ, 256, 128), F32),
             DMA((2, 4, 4)), DMA((2, 4, 4)), DMA((8, 4)), DMA((8, 4)),
-            DMA((3, 8)), DMA((3, 8)), DMA((6,)), DMA, DMA,
+            DMA((6, 8)), DMA((6, 8)), DMA((9,)), DMA((2,)), DMA((2,)),
         ],
         compiler_params=pltpu.CompilerParams(
             collective_id=0, has_side_effects=True, vmem_limit_bytes=60 * 2**20),
         name="gather_project",
-    )(hidden, output_matrix, prefix_page_cache, up, down, weight, gain,
-      lengths, request_adapter, request_prompt, prompt_page_table)
+    )(hidden, output_matrix, prefix_page_cache, adapter_up, jnp.swapaxes(adapter_down, 1, 2),
+      query_key_value_weight.T, attention_scale,
+      lengths, request_adapter, request_prompt, prompt_page_table.T)
     attn = pl.pallas_call(
         attend_kernel,
         out_shape=jax.ShapeDtypeStruct((NT, 64, 128), BF16),
-        in_specs=[VM, VM, VM, SM],
+        in_specs=[VM, VM, SM],
         out_specs=VM,
-        scratch_shapes=[pltpu.VMEM((256, 128), F32)],
+        scratch_shapes=[pltpu.VMEM((256, 128), F32), pltpu.SMEM((2 * NREQ,), jnp.int32)],
         name="attend",
-    )(queries, key_values, prefix, lengths)
-    return pl.pallas_call(
+    )(queries, key_values, lengths)
+    sums, mixed = pl.pallas_call(
         mix_kernel,
-        out_shape=jax.ShapeDtypeStruct((ROWS, D), BF16),
-        in_specs=[VM, HB, VM, HB, HB, HB, VM, VM, VM, VM],
-        out_specs=VM,
+        out_shape=(jax.ShapeDtypeStruct((ROWS, D), F32), jax.ShapeDtypeStruct((ROWS, D), BF16)),
+        in_specs=[VM, HB, VM, HB, HB, HB, VM, VM, VM],
+        out_specs=(VM, VM),
         scratch_shapes=[
             pltpu.VMEM((NT, 64, 128), BF16),
             pltpu.VMEM((ROWS, NT * HW), BF16),
             pltpu.VMEM((NT * HW, D), BF16),
-            pltpu.VMEM((D, 320), BF16),
-            pltpu.VMEM((D, 320), BF16),
+            pltpu.VMEM((320, D), BF16),
+            pltpu.VMEM((320, D), BF16),
             pltpu.VMEM((320, D), BF16),
             pltpu.VMEM((NT, ROWS, D), BF16),
             pltpu.VMEM((NT, ROWS, D), BF16),
             pltpu.VMEM((NZ, ROWS, D), BF16),
             pltpu.VMEM((4, ROWS, D), BF16), pltpu.VMEM((4, ROWS, D), BF16),
             pltpu.VMEM((4, ROWS, D), BF16), pltpu.VMEM((4, ROWS, D), BF16),
-            DMA((16,)), DMA((16,)), DMA((2, 4, 2)), DMA((2, 4, 2)), DMA((8, 2)), DMA((8, 2)),
-            DMA((8,)), DMA((8,)), DMA((2, 4, 2)), DMA((2, 4, 2)), DMA((5,)),
+            DMA((16,)), DMA((16,)), DMA((2, 4, 4)), DMA((2, 4, 4)), DMA((8, 4)), DMA((8, 4)),
+            DMA((8,)), DMA((8,)), DMA((2, 4, 4)), DMA((2, 4, 4)), DMA((5,)),
         ],
         compiler_params=pltpu.CompilerParams(
             collective_id=1, has_side_effects=True, vmem_limit_bytes=60 * 2**20),
         name="mix_feed",
-    )(attn, matrix.reshape(NT * HW, D), hidden, up_matrix, gate_matrix, down_matrix,
-      up_scaling.reshape(1, -1), gate_scaling.reshape(1, -1),
-      attention_rate.reshape(1, -1), feedforward_rate.reshape(1, -1))
+    )(attn, matrix.reshape(NT * HW, D), hidden, up_matrix.T, gate_matrix.T, down_matrix,
+      up_scaling, gate_scaling, attention_rate)
+    return pl.pallas_call(
+        finish_kernel,
+        out_shape=jax.ShapeDtypeStruct((ROWS, D), BF16),
+        in_specs=[VM, VM, VM],
+        out_specs=VM,
+        name="finish",
+    )(sums, mixed, feedforward_rate)
 
 
 def solution(mesh):

time: 160 us -> 141 us (0.88)
  local copies, waits for them, and re-layouts: 9.55 us -> 0 us
  Pallas kernels: 148 us -> 141 us
  other arithmetic: 1.61 us -> 0 us
    pallas_call x1, Pallas kernels: 16.8 us -> 11.1 us  [local(): pl.pallas_call(attend_kernel, out_shape=jax.ShapeDtypeStruct((NT, 64, 128...]
    unnamed x24 -> x0, local copies, waits for them, and re-layouts: 5.49 us -> none
    reshape x5 -> x0, local copies, waits for them, and re-layouts: 2.9 us -> none  [the longest x1 0.6 us: local(): attention_rate.reshape(1, -1)]
    concatenate x2 -> x0, other arithmetic: 1.61 us -> none  [spread(): jnp.concatenate([m[..., :HW], jnp.zeros_like(m[..., :HW]), m[..., HW:]],...]
    pallas_call x1 -> x2, Pallas kernels: 74.2 us -> 73.3 us  [the longest x1 71.1 us: local(): pl.pallas_call(mix_kernel, out_shape=(jax.ShapeDtypeStruct((ROWS, D), F32...]
where the time goes in v2:
time: 141 us
  Pallas kernels  141 us (100%)
    pallas_call x1, Pallas kernels, local(): pl.pallas_call(mix_kernel, out_shape=(jax.ShapeDtypeStruct((ROWS, D), F32...  71.1 us
    pallas_call x1, Pallas kernels, local(): pl.pallas_call(gather_kernel, out_shape=(jax.ShapeDtypeStruct((GROUP, 128...  56.6 us
    pallas_call x1, Pallas kernels, local(): pl.pallas_call(attend_kernel, out_shape=jax.ShapeDtypeStruct((NT, 64, 128...  11.1 us

profile of v2, /device:TPU:1, one launch (start us, length us, event | category | flops | bytes accessed | tf_op | source)
XLA Modules:
  0.0 141.1 jit_solution(5176187104839955159)
XLA Ops:
  0.0 56.6 %gather_project.1 = (bf16[2048,128]{1,0:T(8,128)(2,1)}, bf16[4096,128]{1,0:T(8,128)(2,1)}, bf16[16,64,1280]{2,1,0:T(8,128)(2,1)}) custom-call(bf16[128,1280]{1,0:T(8,128)(2,1)} %h_ref.3, bf16[64,1280]{1,0:T(8,128)(2,1)} %o_ref.1, bf16[4,64,128]{2,1,0:T(8,128)(2,1)} %pg_ref.1, bf16[4,16,192]{2,1,0:T(8,128)(2,1)} %up_ref.1, bf16[4,16,1280]{2,1,0:T(8,128)(2,1)} %bitcast.10, ...), custom_call_target="tpu_custom_call" | custom-call | tf_op jit(solution)/shard_map/gather_project/pallas_call | solution.py:555
  56.7 11.1 %attend.1.attn_ref = bf16[16,64,128]{2,1,0:T(8,128)(2,1)} custom-call(bf16[2048,128]{1,0:T(8,128)(2,1)} %get-tuple-element.10.q_ref, bf16[4096,128]{1,0:T(8,128)(2,1)} %get-tuple-element.11.kv_ref, s32[1,8]{1,0:T(1,128)} %len_ref.3), custom_call_target="tpu_custom_call" | custom-call | tf_op jit(solution)/shard_map/attend/pallas_call | solution.py:585
  67.7 71.1 %mix_feed.1 = (f32[128,1280]{1,0:T(8,128)}, bf16[128,1280]{1,0:T(8,128)(2,1)}) custom-call(bf16[16,64,128]{2,1,0:T(8,128)(2,1)} %attend.1.attn_ref, bf16[1024,1280]{1,0:T(8,128)(2,1)} %bitcast.6, bf16[128,1280]{1,0:T(8,128)(2,1)} %h_ref.3, bf16[320,1280]{1,0:T(8,128)(2,1)} %bitcast.7, bf16[320,1280]{1,0:T(8,128)(2,1)} %bitcast.8, bf16[320,1280]{1,0:T(8,128)(2,1)} %wd_ref.1, ...), custom_call_target="tpu_custom_call" | custom-call | tf_op jit(solution)/shard_map/mix_feed/pallas_call | solution.py:593
  138.8 2.3 %finish.1 = bf16[128,1280]{1,0:T(8,128)(2,1)} custom-call(f32[128,1280]{1,0:T(8,128)} %get-tuple-element.13.sum_ref, bf16[128,1280]{1,0:T(8,128)(2,1)} %get-tuple-element.14.mixed_ref, f32[1280]{0:T(1024)} %rate_ref.1), custom_call_target="tpu_custom_call" | custom-call | tf_op jit(solution)/shard_map/finish/pallas_call | solution.py:618

commit v3 on v2

--- a/solution.py
+++ b/solution.py
@@ -41,27 +41,26 @@
 
 
 class Ring:
-    def __init__(self, chunks, zsend, zrecv, psend, precv):
-        self.dp, self.t, self.z, self.c = place()
+    def __init__(self, chunks, zsend, zrecv, psend=None, precv=None):
+        self.dp, _, self.z, self.c = place()
         self.chunks, self.zsend, self.zrecv = chunks, zsend, zrecv
         self.psend, self.precv = psend, precv
         self.started = []
         self.next = (self.dp, at_z(self.z, 1) * 2 + self.c), (self.dp, at_z(self.z, -1) * 2 + self.c)
         self.other = (self.dp, self.z * 2 + (1 - self.c))
 
-    def spot(self, k, block):
-        buf, _, r0, n = self.chunks[k]
-        return buf.at[block, pl.ds(r0, n)]
-
-    def ring_copy(self, way, step, k, src, block):
+    def spot(self, k, zb, core):
+        return self.chunks[k][0](zb, core)
+
+    def ring_copy(self, way, step, k, src, zb):
         return pltpu.make_async_remote_copy(
-            src_ref=src, dst_ref=self.spot(k, block),
+            src_ref=src, dst_ref=self.spot(k, zb, self.c),
             send_sem=self.zsend.at[way, step - 1, k], recv_sem=self.zrecv.at[way, step - 1, k],
             device_id=self.next[way], device_id_type=MESH)
 
-    def core_copy(self, i, k, src, block):
+    def core_copy(self, i, k, src, zb, core):
         return pltpu.make_async_remote_copy(
-            src_ref=src, dst_ref=self.spot(k, block),
+            src_ref=src, dst_ref=self.spot(k, zb, core),
             send_sem=self.psend.at[i, k], recv_sem=self.precv.at[i, k],
             device_id=self.other, device_id_type=MESH)
 
@@ -69,43 +68,46 @@
         copy.start()
         self.started.append(copy)
 
-    def source(self, k):
-        _, src, r0, n = self.chunks[k]
-        return src.at[pl.ds(r0, n)]
-
-    def first(self):
-        for ks in self.order():
-            for way in range(2):
-                self.go(self.ring_copy(way, 1, ks[way], self.source(ks[way]), self.t))
+    def turn(self, n):
+        count = len(self.chunks)
+        return n, (n + count // 2) % count
+
+    def first(self, ns=None):
+        ns = range(len(self.chunks)) if ns is None else ns
+        for n in ns:
+            for way, k in enumerate(self.turn(n)):
+                self.go(self.ring_copy(way, 1, k, self.chunks[k][1], self.z))
+        if self.psend is not None:
+            for n in ns:
+                self.go(self.core_copy(0, n, self.chunks[n][1], self.z, self.c))
+
+    def step(self, s, ns=None):
+        for n in range(len(self.chunks)) if ns is None else ns:
+            far = n < len(self.chunks) // 2
+            if s == 4 and not far:
+                continue
+            for way, k in enumerate(self.turn(n)):
+                zb = at_z(self.z, -s if way == 0 else s)
+                here = self.spot(k, zb, self.c)
+                self.ring_copy(way, s, k, here, zb).wait_recv()
+                if s < 3 or (s == 3 and far):
+                    self.go(self.ring_copy(way, s + 1, k, here, zb))
+                if self.psend is not None:
+                    i = 7 if s == 4 else (2 * s - 1 if way == 0 else 2 * s)
+                    self.go(self.core_copy(i, k, here, zb, self.c))
+
+    def from_core(self, i):
+        zb = at_z(self.z, delta(i))
         for k in range(len(self.chunks)):
-            self.go(self.core_copy(0, k, self.source(k), self.t))
-
-    def order(self):
-        n = len(self.chunks)
-        return [(k, (k + n // 2) % n) for k in range(n)]
-
-    def step(self, s):
-        for n, ks in enumerate(self.order()):
-            for way in range(2):
-                k, far = ks[way], n < len(self.chunks) // 2
-                if s == 4 and not far:
-                    continue
-                block = at_z(self.z, -s if way == 0 else s) * 2 + self.c
-                here = self.spot(k, block)
-                self.ring_copy(way, s, k, here, block).wait_recv()
-                if s < 3 or (s == 3 and far):
-                    self.go(self.ring_copy(way, s + 1, k, here, block))
-                i = 7 if s == 4 else (2 * s - 1 if way == 0 else 2 * s)
-                self.go(self.core_copy(i, k, here, block))
-
-    def from_core(self, i):
-        block = at_z(self.z, delta(i)) * 2 + (1 - self.c)
-        for k in range(len(self.chunks)):
-            self.core_copy(i, k, self.spot(k, block), block).wait_recv()
+            self.core_copy(i, k, self.spot(k, zb, 1 - self.c), zb, 1 - self.c).wait_recv()
 
     def drain(self):
         for copy in self.started:
             copy.wait_send()
+
+
+def slab(buf, first_row, rows):
+    return lambda zb, core: buf.at[zb * 2 + core, pl.ds(first_row, rows)]
 
 
 class Plane:
@@ -179,6 +181,49 @@
         far = self.buf.at[(self.b + 2) % 4]
         self.got(6, self.halves(far)[0])
         self.got(7, self.halves(far)[1])
+
+    def drain(self):
+        for c in self.started:
+            c.wait_send()
+
+
+class Line:
+    def __init__(self, number, axis, at, send, recv):
+        dp, t, _, _ = place()
+        x, y = dp // 4, dp % 4
+        self.n, self.at, self.send, self.recv = number, at, send, recv
+        self.a = x if axis == 0 else y
+
+        def device(a):
+            return (a * 4 + y if axis == 0 else x * 4 + a), t
+
+        self.lo, self.hi, self.far = (self.a + 3) % 4, (self.a + 1) % 4, (self.a + 2) % 4
+        self.devs = device(self.hi), device(self.lo)
+        self.started = []
+
+    def copy(self, k, ref, dev):
+        return pltpu.make_async_remote_copy(
+            src_ref=ref, dst_ref=ref, send_sem=self.send.at[self.n, k], recv_sem=self.recv.at[self.n, k],
+            device_id=dev, device_id_type=MESH)
+
+    def go(self, k, ref, dev):
+        c = self.copy(k, ref, dev)
+        c.start()
+        self.started.append(c)
+
+    def one(self):
+        for k in range(2):
+            self.go(k, self.at(self.a, 0, 8), self.devs[k])
+
+    def two(self):
+        self.copy(0, self.at(self.lo, 0, 8), self.devs[0]).wait_recv()
+        self.go(2, self.at(self.lo, 0, 4), self.devs[0])
+        self.copy(1, self.at(self.hi, 0, 8), self.devs[1]).wait_recv()
+        self.go(3, self.at(self.hi, 4, 4), self.devs[1])
+
+    def three(self):
+        self.copy(2, self.at(self.far, 0, 4), self.devs[0]).wait_recv()
+        self.copy(3, self.at(self.far, 4, 4), self.devs[1]).wait_recv()
 
     def drain(self):
         for c in self.started:
@@ -212,8 +257,8 @@
 
 def gather_kernel(h_ref, o_ref, pg_ref, up_ref, dn_ref, w_ref, gain_ref, len_ref, ra_ref, rp_ref, pt_ref,
                   q_out, kv_out, o_out,
-                  gh, go, pb, ub, db, wide, sel, tail, su, gains, trig,
-                  zsend, zrecv, psend, precv, xsend, xrecv, local, dsend, drecv):
+                  gh, ob, pb, ub, db, wide, sel, tail, su, gains, trig,
+                  zsend, zrecv, psend, precv, usend, urecv, xsend, xrecv, lsend, lrecv, local, dsend, drecv):
     dp, t, z, c = place()
     x, y = dp // 4, dp % 4
     greet([
@@ -221,25 +266,39 @@
         (((x + 1) % 4) * 4 + y, t), (((x + 3) % 4) * 4 + y, t),
         (x * 4 + (y + 1) % 4, t), (x * 4 + (y + 3) % 4, t),
     ])
-    ring = Ring([(gh, h_ref, 0, 64), (go, o_ref, 0, 32), (gh, h_ref, 64, 64), (go, o_ref, 32, 32)],
+    ring = Ring([(slab(gh, 64 * k, 64), h_ref.at[pl.ds(64 * k, 64)]) for k in range(2)],
                 zsend, zrecv, psend, precv)
+    quarters = [(x, o_ref.at[pl.ds(pl.multiple_of(16 * x, 16), 16), pl.ds(0, D // 2)]),
+                (y, o_ref.at[pl.ds(pl.multiple_of(16 * y, 16), 16), pl.ds(D // 2, D // 2)])]
+    oring = Ring([(functools.partial(lambda part, j, zb, core: ob.at[part, j, zb, core], part, j), src)
+                  for part, (j, src) in enumerate(quarters)], usend, urecv)
+    lines = [Line(part, part, functools.partial(
+        lambda part, j, z0, n: ob.at[part, j, pl.ds(z0, n), c], part), lsend, lrecv) for part in range(2)]
     planes = []
     for half in range(2):
         for src, buf in ((dn_ref.at[2 * c + half], db.at[c, half]),
                          (pg_ref.at[pl.ds(2 * half, 2)], pb.at[half]),
                          (up_ref.at[pl.ds(2 * half, 2)], ub.at[half])):
             planes.append(Plane(len(planes), half, src, buf, xsend, xrecv, local))
-    ring.first()
+    oring.first()
+    ring.first([0])
     for p in planes:
         p.one()
-    own_h = pltpu.make_async_copy(h_ref, gh.at[t], local.at[6])
-    own_h.start()
-    own_o = pltpu.make_async_copy(o_ref, go.at[t], local.at[7])
-    own_o.start()
+    owns = [pltpu.make_async_copy(h_ref, gh.at[t], local.at[6])]
+    for part, (j, src) in enumerate(quarters):
+        owns.append(pltpu.make_async_copy(src, ob.at[part, j, z, c], local.at[7 + part]))
+    for own in owns:
+        own.start()
+    oring.step(1)
+    ring.first([1])
     for p in planes:
         p.two()
     for p in planes:
         p.three()
+    for own in owns:
+        own.wait()
+    oring.step(2)
+    ring.step(1, [0])
 
     lane = lanes((256, 128))
     low = lane < HW
@@ -253,18 +312,24 @@
     frequency = jnp.exp((lane % 32).astype(F32) * (-2.0 * math.log(10000.0) / HW))
     quarter = jnp.where(low, 0.0, 0.5 * math.pi)
 
-    @pl.loop(0, NZ)
-    def _(b):
+    def waves(b):
         rows, _, start = row_starts(len_ref, b * 256, (256, 128))
         angle = (rows - start + PREFIX).astype(F32) * frequency
         trig[b] = jnp.cos(angle - quarter)
 
-    own_h.wait()
-    own_o.wait()
-    ring.step(1)
+    pl.loop(0, 4)(waves)
+    oring.step(3)
+    ring.step(1, [1])
+    pl.loop(4, 8)(waves)
+    oring.step(4)
+    for line in lines:
+        line.one()
+    ring.step(2, [0])
     for p in planes:
         p.four()
-    ring.step(2)
+    ring.step(2, [1])
+    for line in lines:
+        line.two()
     for p in planes:
         p.five()
     swaps = []
@@ -274,6 +339,14 @@
             device_id=(dp, z * 2 + (1 - c)), device_id_type=MESH)
         swap.start()
         swaps.append(swap)
+
+    for line in lines:
+        line.three()
+    matrix_swap = pltpu.make_async_remote_copy(
+        src_ref=ob.at[:, :, :, c], dst_ref=ob.at[:, :, :, c], send_sem=dsend.at[2], recv_sem=drecv.at[2],
+        device_id=(dp, z * 2 + (1 - c)), device_id_type=MESH)
+    matrix_swap.start()
+    swaps.append(matrix_swap)
 
     def unit(v):
         total = jnp.sum(jnp.where(low, v * v, 0.0), axis=1, keepdims=True)
@@ -341,13 +414,15 @@
     pl.loop(0, 3)(project)
     ring.step(3)
     pl.loop(3, 5)(project)
+    pltpu.make_async_remote_copy(
+        src_ref=ob.at[:, :, :, 1 - c], dst_ref=ob.at[:, :, :, 1 - c], send_sem=dsend.at[2], recv_sem=drecv.at[2],
+        device_id=(dp, z * 2 + (1 - c)), device_id_type=MESH).wait_recv()
+    out = pltpu.make_async_copy(ob, o_out, local.at[9])
+    out.start()
     ring.step(4)
     pl.loop(5, 8)(project)
-    out = pltpu.make_async_copy(go, o_out, local.at[8])
-    out.start()
-    ring.drain()
-    for p in planes:
-        p.drain()
+    for part in [ring, oring] + planes + lines:
+        part.drain()
     for swap in swaps:
         swap.wait_send()
     out.wait()
@@ -427,10 +502,11 @@
             device_id=(dp, to), device_id_type=MESH)
         copy.start()
         started.append(copy)
-    own = pltpu.make_async_copy(attn_ref.at[t], heads.at[t], local.at[4])
+    own = pltpu.make_async_copy(attn_ref.at[t], heads.at[t], local.at[11])
     own.start()
-    loads = [pltpu.make_async_copy(a, b, local.at[n])
-             for n, (a, b) in enumerate([(o_ref, om), (wu_ref, wu), (wg_ref, wg), (wd_ref, wd)])]
+    moves = [(o_ref.at[part, j], om.at[:, :, j, :, pl.ds(part * (D // 2), D // 2)])
+             for part in range(2) for j in range(4)] + [(wu_ref, wu), (wg_ref, wg), (wd_ref, wd)]
+    loads = [pltpu.make_async_copy(a, b, local.at[n]) for n, (a, b) in enumerate(moves)]
     for copy in loads:
         copy.start()
     base = h_ref[...].astype(F32)
@@ -446,15 +522,16 @@
         cols = slice(128 * j, 128 * j + 128)
         lhs[0:64, cols] = jnp.where(high, odd, pltpu.roll(even, HW, 1)).astype(BF16)
         lhs[64:128, cols] = jnp.where(high, pltpu.roll(odd, HW, 1), even).astype(BF16)
-    loads[0].wait()
-    attn_sum = jnp.dot(lhs[...], om[...], preferred_element_type=F32)
+    for copy in loads[:8]:
+        copy.wait()
+    attn_sum = jnp.dot(lhs[...], om[...].reshape(NT * HW, D), preferred_element_type=F32)
     rate = ra_ref[...].reshape(1, D)
     mine = renorm(base + rate * (renorm(attn_sum) - base)).astype(BF16)
     mixed[t] = mine
-    ring = Ring([(mixed, mixed.at[t], 32 * k, 32) for k in range(4)], zsend, zrecv, psend, precv)
+    ring = Ring([(slab(mixed, 32 * k, 32), mixed.at[t, pl.ds(32 * k, 32)]) for k in range(4)], zsend, zrecv, psend, precv)
     ring.first()
     mixed_out[...] = mine
-    for copy in loads[1:]:
+    for copy in loads[8:]:
         copy.wait()
     scale_up, scale_gate = su_ref[...].reshape(1, 320), sg_ref[...].reshape(1, 320)
 
@@ -557,13 +634,13 @@
         out_shape=(
             jax.ShapeDtypeStruct((GROUP, 128), BF16),
             jax.ShapeDtypeStruct((NREQ * PREFIX + GROUP, 128), BF16),
-            jax.ShapeDtypeStruct((NT, HW, D), BF16),
+            jax.ShapeDtypeStruct((2, 4, NZ, 2, 16, D // 2), BF16),
         ),
         in_specs=[HB, HB, HB, HB, HB, VM, VM, SM, SM, SM, SM],
         out_specs=(VM, VM, HB),
         scratch_shapes=[
             pltpu.VMEM((NT, ROWS, D), BF16),
-            pltpu.VMEM((NT, HW, D), BF16),
+            pltpu.VMEM((2, 4, NZ, 2, 16, D // 2), BF16),
             pltpu.VMEM((2, 4, 4, 2, 64, 128), BF16),
             pltpu.VMEM((2, 4, 4, 2, RANK, 192), BF16),
             pltpu.VMEM((2, 2, 4, 4, RANK, D), BF16),
@@ -573,8 +650,8 @@
             pltpu.VMEM((128, 256), BF16),
             pltpu.VMEM((8, 128), F32),
             pltpu.VMEM((NZ, 256, 128), F32),
-            DMA((2, 4, 4)), DMA((2, 4, 4)), DMA((8, 4)), DMA((8, 4)),
-            DMA((6, 8)), DMA((6, 8)), DMA((9,)), DMA((2,)), DMA((2,)),
+            DMA((2, 4, 2)), DMA((2, 4, 2)), DMA((8, 2)), DMA((8, 2)), DMA((2, 4, 2)), DMA((2, 4, 2)),
+            DMA((6, 8)), DMA((6, 8)), DMA((2, 4)), DMA((2, 4)), DMA((10,)), DMA((3,)), DMA((3,)),
         ],
         compiler_params=pltpu.CompilerParams(
             collective_id=0, has_side_effects=True, vmem_limit_bytes=60 * 2**20),
@@ -598,7 +675,7 @@
         scratch_shapes=[
             pltpu.VMEM((NT, 64, 128), BF16),
             pltpu.VMEM((ROWS, NT * HW), BF16),
-            pltpu.VMEM((NT * HW, D), BF16),
+            pltpu.VMEM((NZ, 2, 4, 16, D), BF16),
             pltpu.VMEM((320, D), BF16),
             pltpu.VMEM((320, D), BF16),
             pltpu.VMEM((320, D), BF16),
@@ -608,12 +685,12 @@
             pltpu.VMEM((4, ROWS, D), BF16), pltpu.VMEM((4, ROWS, D), BF16),
             pltpu.VMEM((4, ROWS, D), BF16), pltpu.VMEM((4, ROWS, D), BF16),
             DMA((16,)), DMA((16,)), DMA((2, 4, 4)), DMA((2, 4, 4)), DMA((8, 4)), DMA((8, 4)),
-            DMA((8,)), DMA((8,)), DMA((2, 4, 4)), DMA((2, 4, 4)), DMA((5,)),
+            DMA((8,)), DMA((8,)), DMA((2, 4, 4)), DMA((2, 4, 4)), DMA((12,)),
         ],
         compiler_params=pltpu.CompilerParams(
             collective_id=1, has_side_effects=True, vmem_limit_bytes=60 * 2**20),
         name="mix_feed",
-    )(attn, matrix.reshape(NT * HW, D), hidden, up_matrix.T, gate_matrix.T, down_matrix,
+    )(attn, matrix, hidden, up_matrix.T, gate_matrix.T, down_matrix,
       up_scaling, gate_scaling, attention_rate)
     return pl.pallas_call(
         finish_kernel,

time: 141 us -> 140 us (level)
    pallas_call x1, Pallas kernels: 56.6 us -> 53.2 us  [local(): pl.pallas_call(gather_kernel, out_shape=(jax.ShapeDtypeStruct((GROUP, 128...]
where the time goes in v3:
time: 140 us
  Pallas kernels  140 us (100%)
    pallas_call x1, Pallas kernels, local(): pl.pallas_call(mix_kernel, out_shape=(jax.ShapeDtypeStruct((ROWS, D), F32...  72.2 us
    pallas_call x1, Pallas kernels, local(): pl.pallas_call(gather_kernel, out_shape=(jax.ShapeDtypeStruct((GROUP, 128...  53.2 us
    pallas_call x1, Pallas kernels, local(): pl.pallas_call(attend_kernel, out_shape=jax.ShapeDtypeStruct((NT, 64, 128...  12.2 us

profile of v3, /device:TPU:1, one launch (start us, length us, event | category | flops | bytes accessed | tf_op | source)
XLA Modules:
  0.0 140.0 jit_solution(3122357116940571428)
XLA Ops:
  0.0 53.2 %gather_project.1 = (bf16[2048,128]{1,0:T(8,128)(2,1)}, bf16[4096,128]{1,0:T(8,128)(2,1)}, bf16[2,4,8,2,16,640]{5,4,3,2,1,0:T(8,128)(2,1)}) custom-call(bf16[128,1280]{1,0:T(8,128)(2,1)} %h_ref.3, bf16[64,1280]{1,0:T(8,128)(2,1)} %o_ref.1, bf16[4,64,128]{2,1,0:T(8,128)(2,1)} %pg_ref.1, bf16[4,16,192]{2,1,0:T(8,128)(2,1)} %up_ref.1, ...), custom_call_target="tpu_custom_call" | custom-call | tf_op jit(solution)/shard_map/gather_project/pallas_call | solution.py:632
  53.2 12.2 %attend.1.attn_ref = bf16[16,64,128]{2,1,0:T(8,128)(2,1)} custom-call(bf16[2048,128]{1,0:T(8,128)(2,1)} %get-tuple-element.10.q_ref, bf16[4096,128]{1,0:T(8,128)(2,1)} %get-tuple-element.11.kv_ref, s32[1,8]{1,0:T(1,128)} %len_ref.3), custom_call_target="tpu_custom_call" | custom-call | tf_op jit(solution)/shard_map/attend/pallas_call | solution.py:662
  65.4 72.2 %mix_feed.1 = (f32[128,1280]{1,0:T(8,128)}, bf16[128,1280]{1,0:T(8,128)(2,1)}) custom-call(bf16[16,64,128]{2,1,0:T(8,128)(2,1)} %attend.1.attn_ref, bf16[2,4,8,2,16,640]{5,4,3,2,1,0:T(8,128)(2,1)} %get-tuple-element.12.o_ref, bf16[128,1280]{1,0:T(8,128)(2,1)} %h_ref.3, bf16[320,1280]{1,0:T(8,128)(2,1)} %bitcast.5, bf16[320,1280]{1,0:T(8,128)(2,1)} %bitcast.6, ...), custom_call_target="tpu_custom_call" | custom-call | tf_op jit(solution)/shard_map/mix_feed/pallas_call | solution.py:670
  137.7 2.3 %finish.1 = bf16[128,1280]{1,0:T(8,128)(2,1)} custom-call(f32[128,1280]{1,0:T(8,128)} %get-tuple-element.13.sum_ref, bf16[128,1280]{1,0:T(8,128)(2,1)} %get-tuple-element.14.mixed_ref, f32[1280]{0:T(1024)} %rate_ref.1), custom_call_target="tpu_custom_call" | custom-call | tf_op jit(solution)/shard_map/finish/pallas_call | solution.py:695

commit v4 on v3

--- a/solution.py
+++ b/solution.py
@@ -166,6 +166,8 @@
         self.got(2, self.halves(far)[0])
         self.got(3, self.halves(far)[1])
         self.own.wait()
+
+    def turn(self):
         row = self.buf.at[self.b]
         self.go(4, row, row, self.dev_b[0])
         self.go(5, row, row, self.dev_b[1])
@@ -256,8 +258,8 @@
 
 
 def gather_kernel(h_ref, o_ref, pg_ref, up_ref, dn_ref, w_ref, gain_ref, len_ref, ra_ref, rp_ref, pt_ref,
-                  q_out, kv_out, o_out,
-                  gh, ob, pb, ub, db, wide, sel, tail, su, gains, trig,
+                  q_out, kv_out, ob,
+                  gh, pb, ub, db, wide, sel, tail, su, gains, trig,
                   zsend, zrecv, psend, precv, usend, urecv, xsend, xrecv, lsend, lrecv, local, dsend, drecv):
     dp, t, z, c = place()
     x, y = dp // 4, dp % 4
@@ -274,12 +276,12 @@
                   for part, (j, src) in enumerate(quarters)], usend, urecv)
     lines = [Line(part, part, functools.partial(
         lambda part, j, z0, n: ob.at[part, j, pl.ds(z0, n), c], part), lsend, lrecv) for part in range(2)]
-    planes = []
+    adapters, pages = [], []
     for half in range(2):
-        for src, buf in ((dn_ref.at[2 * c + half], db.at[c, half]),
-                         (pg_ref.at[pl.ds(2 * half, 2)], pb.at[half]),
-                         (up_ref.at[pl.ds(2 * half, 2)], ub.at[half])):
-            planes.append(Plane(len(planes), half, src, buf, xsend, xrecv, local))
+        adapters.append(Plane(half, half, dn_ref.at[2 * c + half], db.at[c, half], xsend, xrecv, local))
+        adapters.append(Plane(2 + half, half, up_ref.at[pl.ds(2 * half, 2)], ub.at[half], xsend, xrecv, local))
+        pages.append(Plane(4 + half, half, pg_ref.at[pl.ds(2 * half, 2)], pb.at[half], xsend, xrecv, local))
+    planes = adapters + pages
     oring.first()
     ring.first([0])
     for p in planes:
@@ -287,14 +289,19 @@
     owns = [pltpu.make_async_copy(h_ref, gh.at[t], local.at[6])]
     for part, (j, src) in enumerate(quarters):
         owns.append(pltpu.make_async_copy(src, ob.at[part, j, z, c], local.at[7 + part]))
+    owns.append(pltpu.make_async_copy(
+        w_ref.at[pl.ds(0, HW)], wide.at[pl.ds(128, HW)], local.at[9]))
+    owns.append(pltpu.make_async_copy(
+        w_ref.at[pl.ds(HW, 2 * HW)], wide.at[pl.ds(256, 2 * HW)], local.at[10]))
     for own in owns:
         own.start()
     oring.step(1)
     ring.first([1])
     for p in planes:
         p.two()
-    for p in planes:
+    for p in adapters:
         p.three()
+        p.turn()
     for own in owns:
         own.wait()
     oring.step(2)
@@ -305,9 +312,7 @@
     gains[...] = jnp.ones_like(gains)
     gains[:, 0:HW] = jnp.broadcast_to(gain_ref[...].reshape(1, HW), (8, HW))
     gain = gains[0:1, :]
-    wide[128:192, :] = w_ref[0:HW, :]
     wide[192:256, :] = jnp.zeros((HW, D), BF16)
-    wide[256:384, :] = w_ref[HW:3 * HW, :]
     tail[...] = jnp.zeros_like(tail)
     frequency = jnp.exp((lane % 32).astype(F32) * (-2.0 * math.log(10000.0) / HW))
     quarter = jnp.where(low, 0.0, 0.5 * math.pi)
@@ -318,35 +323,34 @@
         trig[b] = jnp.cos(angle - quarter)
 
     pl.loop(0, 4)(waves)
+    for p in pages:
+        p.three()
     oring.step(3)
     ring.step(1, [1])
+    for p in adapters:
+        p.four()
+    for p in pages:
+        p.turn()
     pl.loop(4, 8)(waves)
+    for p in adapters:
+        p.five()
+    other = (dp, z * 2 + (1 - c))
+
+    def to_other(n, mine, theirs):
+        send = pltpu.make_async_remote_copy(
+            src_ref=mine, dst_ref=mine, send_sem=dsend.at[n], recv_sem=drecv.at[n],
+            device_id=other, device_id_type=MESH)
+        receive = pltpu.make_async_remote_copy(
+            src_ref=theirs, dst_ref=theirs, send_sem=dsend.at[n], recv_sem=drecv.at[n],
+            device_id=other, device_id_type=MESH)
+        send.start()
+        return send, receive
+
+    swaps = [to_other(half, db.at[c, half], db.at[1 - c, half]) for half in range(2)]
     oring.step(4)
     for line in lines:
         line.one()
     ring.step(2, [0])
-    for p in planes:
-        p.four()
-    ring.step(2, [1])
-    for line in lines:
-        line.two()
-    for p in planes:
-        p.five()
-    swaps = []
-    for half in range(2):
-        swap = pltpu.make_async_remote_copy(
-            src_ref=db.at[c, half], dst_ref=db.at[c, half], send_sem=dsend.at[half], recv_sem=drecv.at[half],
-            device_id=(dp, z * 2 + (1 - c)), device_id_type=MESH)
-        swap.start()
-        swaps.append(swap)
-
-    for line in lines:
-        line.three()
-    matrix_swap = pltpu.make_async_remote_copy(
-        src_ref=ob.at[:, :, :, c], dst_ref=ob.at[:, :, :, c], send_sem=dsend.at[2], recv_sem=drecv.at[2],
-        device_id=(dp, z * 2 + (1 - c)), device_id_type=MESH)
-    matrix_swap.start()
-    swaps.append(matrix_swap)
 
     def unit(v):
         total = jnp.sum(jnp.where(low, v * v, 0.0), axis=1, keepdims=True)
@@ -356,8 +360,7 @@
         a, b = owner // 4, owner % 4
         return b + half * (a - b), a + half * (b - a)
 
-    @pl.loop(0, NREQ)
-    def _(r):
+    def prefix(r):
         prompt = rp_ref[0, r]
         for j in range(4):
             page = pt_ref[j, prompt]
@@ -370,11 +373,8 @@
             kv_out[pl.ds(pl.multiple_of(r * PREFIX + j * 64, 64), 64), :] = jnp.where(
                 low_p, unit_key, raw).astype(BF16)
 
-    for half in range(2):
-        pltpu.make_async_remote_copy(
-            src_ref=db.at[1 - c, half], dst_ref=db.at[1 - c, half],
-            send_sem=dsend.at[half], recv_sem=drecv.at[half],
-            device_id=(dp, z * 2 + (1 - c)), device_id_type=MESH).wait_recv()
+    for _, receive in swaps:
+        receive.wait_recv()
     for r in range(NREQ):
         adapter = ra_ref[0, r]
         within = adapter % 4
@@ -411,21 +411,30 @@
         kv_out[pl.ds(row + NREQ * PREFIX, 256), :] = jnp.where(
             low, unit(rotate(key_value)), key_value).astype(BF16)
 
-    pl.loop(0, 3)(project)
-    ring.step(3)
-    pl.loop(3, 5)(project)
-    pltpu.make_async_remote_copy(
-        src_ref=ob.at[:, :, :, 1 - c], dst_ref=ob.at[:, :, :, 1 - c], send_sem=dsend.at[2], recv_sem=drecv.at[2],
-        device_id=(dp, z * 2 + (1 - c)), device_id_type=MESH).wait_recv()
-    out = pltpu.make_async_copy(ob, o_out, local.at[9])
-    out.start()
+    pl.loop(0, 1)(project)
+    ring.step(2, [1])
+    pl.loop(1, 2)(project)
+    for p in pages:
+        p.four()
+    pl.loop(2, 3)(project)
+    ring.step(3, [0])
+    for line in lines:
+        line.two()
+    pl.loop(3, 4)(project)
+    ring.step(3, [1])
+    for p in pages:
+        p.five()
+    pl.loop(4, 5)(project)
+    pl.loop(0, NREQ)(prefix)
+    pl.loop(5, 6)(project)
     ring.step(4)
-    pl.loop(5, 8)(project)
+    pl.loop(6, 8)(project)
+    for line in lines:
+        line.three()
     for part in [ring, oring] + planes + lines:
         part.drain()
-    for swap in swaps:
-        swap.wait_send()
-    out.wait()
+    for send, _ in swaps:
+        send.wait_send()
 
 
 TILES = 2
@@ -490,7 +499,7 @@
 
 def mix_kernel(attn_ref, o_ref, h_ref, wu_ref, wg_ref, wd_ref, su_ref, sg_ref, ra_ref, sum_out, mixed_out,
                heads, lhs, om, wu, wg, wd, mixed, part, peer, rr, rl, sr, sl,
-               asend, arecv, zsend, zrecv, psend, precv, qsend, qrecv, rsend, rrecv, local):
+               asend, arecv, msend, mrecv, zsend, zrecv, psend, precv, qsend, qrecv, rsend, rrecv, local):
     dp, t, z, c = place()
     greet([(dp, (t + n) % NT) for n in range(1, NT)])
     started = []
@@ -504,8 +513,23 @@
         started.append(copy)
     own = pltpu.make_async_copy(attn_ref.at[t], heads.at[t], local.at[11])
     own.start()
-    moves = [(o_ref.at[part, j], om.at[:, :, j, :, pl.ds(part * (D // 2), D // 2)])
-             for part in range(2) for j in range(4)] + [(wu_ref, wu), (wg_ref, wg), (wd_ref, wd)]
+    eighths = [(part, j) for part in range(2) for j in range(4)]
+
+    def place_in(part, j, core):
+        return om.at[:, core, j, :, pl.ds(part * (D // 2), D // 2)]
+
+    def matrix_copy(n, core):
+        part, j = eighths[n]
+        return pltpu.make_async_remote_copy(
+            src_ref=o_ref.at[part, j, :, c], dst_ref=place_in(part, j, core), send_sem=msend.at[n],
+            recv_sem=mrecv.at[n], device_id=(dp, z * 2 + (1 - c)), device_id_type=MESH)
+
+    for n in range(8):
+        copy = matrix_copy(n, c)
+        copy.start()
+        started.append(copy)
+    moves = [(o_ref.at[part, j, :, c], place_in(part, j, c)) for part, j in eighths]
+    moves += [(wu_ref, wu), (wg_ref, wg), (wd_ref, wd)]
     loads = [pltpu.make_async_copy(a, b, local.at[n]) for n, (a, b) in enumerate(moves)]
     for copy in loads:
         copy.start()
@@ -522,8 +546,9 @@
         cols = slice(128 * j, 128 * j + 128)
         lhs[0:64, cols] = jnp.where(high, odd, pltpu.roll(even, HW, 1)).astype(BF16)
         lhs[64:128, cols] = jnp.where(high, pltpu.roll(odd, HW, 1), even).astype(BF16)
-    for copy in loads[:8]:
-        copy.wait()
+    for n in range(8):
+        loads[n].wait()
+        matrix_copy(n, 1 - c).wait_recv()
     attn_sum = jnp.dot(lhs[...], om[...].reshape(NT * HW, D), preferred_element_type=F32)
     rate = ra_ref[...].reshape(1, D)
     mine = renorm(base + rate * (renorm(attn_sum) - base)).astype(BF16)
@@ -626,21 +651,29 @@
 DMA = pltpu.SemaphoreType.DMA
 
 
+def stay(array):
+    return pltpu.with_memory_space_constraint(array, pltpu.VMEM)
+
+
+def far(array):
+    return pltpu.with_memory_space_constraint(array, pltpu.HBM)
+
+
 def local(hidden, lengths, request_prompt, request_adapter, prompt_page_table, prefix_page_cache,
           query_key_value_weight, adapter_down, adapter_up, attention_scale, output_matrix, attention_rate,
           up_matrix, gate_matrix, up_scaling, gate_scaling, down_matrix, feedforward_rate):
+    lengths = far(lengths)
     queries, key_values, matrix = pl.pallas_call(
         gather_kernel,
         out_shape=(
-            jax.ShapeDtypeStruct((GROUP, 128), BF16),
-            jax.ShapeDtypeStruct((NREQ * PREFIX + GROUP, 128), BF16),
-            jax.ShapeDtypeStruct((2, 4, NZ, 2, 16, D // 2), BF16),
+            pltpu.VMEM((GROUP, 128), BF16),
+            pltpu.VMEM((NREQ * PREFIX + GROUP, 128), BF16),
+            pltpu.VMEM((2, 4, NZ, 2, 16, D // 2), BF16),
         ),
-        in_specs=[HB, HB, HB, HB, HB, VM, VM, SM, SM, SM, SM],
-        out_specs=(VM, VM, HB),
+        in_specs=[HB, HB, HB, HB, HB, HB, VM, SM, SM, SM, SM],
+        out_specs=(VM, VM, VM),
         scratch_shapes=[
             pltpu.VMEM((NT, ROWS, D), BF16),
-            pltpu.VMEM((2, 4, NZ, 2, 16, D // 2), BF16),
             pltpu.VMEM((2, 4, 4, 2, 64, 128), BF16),
             pltpu.VMEM((2, 4, 4, 2, RANK, 192), BF16),
             pltpu.VMEM((2, 2, 4, 4, RANK, D), BF16),
@@ -651,26 +684,28 @@
             pltpu.VMEM((8, 128), F32),
             pltpu.VMEM((NZ, 256, 128), F32),
             DMA((2, 4, 2)), DMA((2, 4, 2)), DMA((8, 2)), DMA((8, 2)), DMA((2, 4, 2)), DMA((2, 4, 2)),
-            DMA((6, 8)), DMA((6, 8)), DMA((2, 4)), DMA((2, 4)), DMA((10,)), DMA((3,)), DMA((3,)),
+            DMA((6, 8)), DMA((6, 8)), DMA((2, 4)), DMA((2, 4)), DMA((11,)), DMA((2,)), DMA((2,)),
         ],
         compiler_params=pltpu.CompilerParams(
-            collective_id=0, has_side_effects=True, vmem_limit_bytes=60 * 2**20),
+            collective_id=0, has_side_effects=True, vmem_limit_bytes=32 * 2**20),
         name="gather_project",
-    )(hidden, output_matrix, prefix_page_cache, adapter_up, jnp.swapaxes(adapter_down, 1, 2),
-      query_key_value_weight.T, attention_scale,
-      lengths, request_adapter, request_prompt, prompt_page_table.T)
+    )(*[far(a) for a in (
+        hidden, output_matrix, prefix_page_cache, adapter_up, jnp.swapaxes(adapter_down, 1, 2),
+        query_key_value_weight.T, attention_scale)],
+      lengths, *[far(a) for a in (request_adapter, request_prompt, prompt_page_table.T)])
     attn = pl.pallas_call(
         attend_kernel,
-        out_shape=jax.ShapeDtypeStruct((NT, 64, 128), BF16),
+        out_shape=pltpu.VMEM((NT, 64, 128), BF16),
         in_specs=[VM, VM, SM],
         out_specs=VM,
         scratch_shapes=[pltpu.VMEM((256, 128), F32), pltpu.SMEM((2 * NREQ,), jnp.int32)],
+        compiler_params=pltpu.CompilerParams(vmem_limit_bytes=16 * 2**20),
         name="attend",
-    )(queries, key_values, lengths)
+    )(stay(queries), stay(key_values), lengths)
     sums, mixed = pl.pallas_call(
         mix_kernel,
-        out_shape=(jax.ShapeDtypeStruct((ROWS, D), F32), jax.ShapeDtypeStruct((ROWS, D), BF16)),
-        in_specs=[VM, HB, VM, HB, HB, HB, VM, VM, VM],
+        out_shape=(pltpu.VMEM((ROWS, D), F32), pltpu.VMEM((ROWS, D), BF16)),
+        in_specs=[VM, VM, VM, HB, HB, HB, VM, VM, VM],
         out_specs=(VM, VM),
         scratch_shapes=[
             pltpu.VMEM((NT, 64, 128), BF16),
@@ -684,21 +719,23 @@
             pltpu.VMEM((NZ, ROWS, D), BF16),
             pltpu.VMEM((4, ROWS, D), BF16), pltpu.VMEM((4, ROWS, D), BF16),
             pltpu.VMEM((4, ROWS, D), BF16), pltpu.VMEM((4, ROWS, D), BF16),
-            DMA((16,)), DMA((16,)), DMA((2, 4, 4)), DMA((2, 4, 4)), DMA((8, 4)), DMA((8, 4)),
+            DMA((16,)), DMA((16,)), DMA((8,)), DMA((8,)),
+            DMA((2, 4, 4)), DMA((2, 4, 4)), DMA((8, 4)), DMA((8, 4)),
             DMA((8,)), DMA((8,)), DMA((2, 4, 4)), DMA((2, 4, 4)), DMA((12,)),
         ],
         compiler_params=pltpu.CompilerParams(
-            collective_id=1, has_side_effects=True, vmem_limit_bytes=60 * 2**20),
+            collective_id=1, has_side_effects=True, vmem_limit_bytes=44 * 2**20),
         name="mix_feed",
-    )(attn, matrix, hidden, up_matrix.T, gate_matrix.T, down_matrix,
+    )(stay(attn), stay(matrix), hidden, up_matrix.T, gate_matrix.T, down_matrix,
       up_scaling, gate_scaling, attention_rate)
     return pl.pallas_call(
         finish_kernel,
         out_shape=jax.ShapeDtypeStruct((ROWS, D), BF16),
         in_specs=[VM, VM, VM],
         out_specs=VM,
+        compiler_params=pltpu.CompilerParams(vmem_limit_bytes=16 * 2**20),
         name="finish",
-    )(sums, mixed, feedforward_rate)
+    )(stay(sums), stay(mixed), feedforward_rate)
 
 
 def solution(mesh):

time: 140 us -> 129 us (0.921)
  Pallas kernels: 140 us -> 129 us
    pallas_call x3, Pallas kernels: 138 us -> 128 us  [the longest x1 73.2 us: local(): pl.pallas_call(mix_kernel, out_shape=(pltpu.VMEM((ROWS, D), F32), pltpu.V...]
where the time goes in v4:
time: 129 us
  Pallas kernels  129 us (100%)
    pallas_call x1, Pallas kernels, local(): pl.pallas_call(mix_kernel, out_shape=(pltpu.VMEM((ROWS, D), F32), pltpu.V...  73.2 us
    pallas_call x1, Pallas kernels, local(): pl.pallas_call(gather_kernel, out_shape=(pltpu.VMEM((GROUP, 128), BF16),...  44.5 us
    pallas_call x1, Pallas kernels, local(): pl.pallas_call(attend_kernel, out_shape=pltpu.VMEM((NT, 64, 128), BF16),...  10 us

profile of v4, /device:TPU:1, one launch (start us, length us, event | category | flops | bytes accessed | tf_op | source)
XLA Modules:
  0.0 128.9 jit_solution(11528760521959012448)
XLA Ops:
  0.0 0.0 copy-start
  0.0 0.0 copy-start.3
  0.0 0.0 copy-start.7
  0.0 0.0 copy-start.6
  0.0 0.0 copy-start.2
  0.0 0.0 copy-start.1
  0.0 0.0 copy-start.4
  0.0 44.5 %gather_project.1 = (bf16[2048,128]{1,0:T(8,128)(2,1)S(1)}, bf16[4096,128]{1,0:T(8,128)(2,1)S(1)}, bf16[2,4,8,2,16,640]{5,4,3,2,1,0:T(8,128)(2,1)S(1)}) custom-call(bf16[128,1280]{1,0:T(8,128)(2,1)} %h_ref.3, bf16[64,1280]{1,0:T(8,128)(2,1)} %o_ref.1, bf16[4,64,128]{2,1,0:T(8,128)(2,1)} %pg_ref.1, bf16[4,16,192]{2,1,0:T(8,128)(2,1)} %up_ref.1, ...), custom_call_target="tpu_custom_call" | custom-call | tf_op jit(solution)/shard_map/gather_project/pallas_call | solution.py:666
  44.5 10.0 %attend.1.attn_ref = bf16[16,64,128]{2,1,0:T(8,128)(2,1)S(1)} custom-call(bf16[2048,128]{1,0:T(8,128)(2,1)S(1)} %get-tuple-element.10.q_ref, bf16[4096,128]{1,0:T(8,128)(2,1)S(1)} %get-tuple-element.11.kv_ref, s32[1,8]{1,0:T(1,128)} %len_ref.3), custom_call_target="tpu_custom_call" | custom-call | tf_op jit(solution)/shard_map/attend/pallas_call | solution.py:696
  54.6 0.0 copy-done
  54.6 0.0 copy-done.3
  54.6 0.0 copy-done.7
  54.6 0.0 copy-done.6
  54.6 0.0 copy-done.2
  54.6 0.0 copy-done.1
  54.6 0.0 copy-done.4
  54.6 0.0 copy-start.5
  54.7 73.2 %mix_feed.1 = (f32[128,1280]{1,0:T(8,128)S(1)}, bf16[128,1280]{1,0:T(8,128)(2,1)S(1)}) custom-call(bf16[16,64,128]{2,1,0:T(8,128)(2,1)S(1)} %attend.1.attn_ref, bf16[2,4,8,2,16,640]{5,4,3,2,1,0:T(8,128)(2,1)S(1)} %get-tuple-element.12.o_ref, bf16[128,1280]{1,0:T(8,128)(2,1)S(1)} %copy-done, bf16[320,1280]{1,0:T(8,128)(2,1)S(1)} %bitcast.5, ...), custom_call_target="tpu_custom_call" | custom-call | tf_op jit(solution)/shard_map/mix_feed/pallas_call | solution.py:705
  127.8 0.0 copy-done.5
  127.8 1.1 finish.1
Async XLA Ops:
  0.0 54.6 %copy-start = (bf16[128,1280]{1,0:T(8,128)(2,1)S(1)}, bf16[128,1280]{1,0:T(8,128)(2,1)}, u32[]{:S(2)}) copy-start(bf16[128,1280]{1,0:T(8,128)(2,1)} %h_ref.3) | copy-start | bytes 983044
  0.0 54.6 %copy-start.3 = (bf16[320,1280]{1,0:T(8,128)(2,1)S(1)}, bf16[320,1280]{1,0:T(8,128)(2,1)}, u32[]{:S(2)}) copy-start(bf16[320,1280]{1,0:T(8,128)(2,1)} %wd_ref.1) | copy-start | bytes 2457604
  0.0 54.6 %copy-start.7 = (f32[320]{0:T(512)S(1)}, f32[320]{0:T(512)}, u32[]{:S(2)}) copy-start(f32[320]{0:T(512)} %sg_ref.1) | copy-start | bytes 3844
  0.0 54.6 %copy-start.6 = (f32[320]{0:T(512)S(1)}, f32[320]{0:T(512)}, u32[]{:S(2)}) copy-start(f32[320]{0:T(512)} %su_ref.1) | copy-start | bytes 3844
  0.0 54.6 %copy-start.2 = (bf16[1280,320]{0,1:T(8,128)(2,1)S(1)}, bf16[1280,320]{0,1:T(8,128)(2,1)}, u32[]{:S(2)}) copy-start(bf16[1280,320]{0,1:T(8,128)(2,1)} %param.31) | copy-start | bytes 2457604
  0.0 54.6 %copy-start.1 = (bf16[1280,320]{0,1:T(8,128)(2,1)S(1)}, bf16[1280,320]{0,1:T(8,128)(2,1)}, u32[]{:S(2)}) copy-start(bf16[1280,320]{0,1:T(8,128)(2,1)} %param.30) | copy-start | bytes 2457604
  0.0 54.6 %copy-start.4 = (f32[1280]{0:T(1024)S(1)}, f32[1280]{0:T(1024)}, u32[]{:S(2)}) copy-start(f32[1280]{0:T(1024)} %ra_ref.3) | copy-start | bytes 15364
  54.6 73.2 %copy-start.5 = (f32[1280]{0:T(1024)S(1)}, f32[1280]{0:T(1024)}, u32[]{:S(2)}) copy-start(f32[1280]{0:T(1024)} %rate_ref.1) | copy-start | bytes 15364

commit v5 on v4

--- a/solution.py
+++ b/solution.py
@@ -41,10 +41,10 @@
 
 
 class Ring:
-    def __init__(self, chunks, zsend, zrecv, psend=None, precv=None):
+    def __init__(self, chunks, zsend, zrecv, psend=None, precv=None, in_order=False):
         self.dp, _, self.z, self.c = place()
         self.chunks, self.zsend, self.zrecv = chunks, zsend, zrecv
-        self.psend, self.precv = psend, precv
+        self.psend, self.precv, self.in_order = psend, precv, in_order
         self.started = []
         self.next = (self.dp, at_z(self.z, 1) * 2 + self.c), (self.dp, at_z(self.z, -1) * 2 + self.c)
         self.other = (self.dp, self.z * 2 + (1 - self.c))
@@ -69,8 +69,13 @@
         self.started.append(copy)
 
     def turn(self, n):
-        count = len(self.chunks)
-        return n, (n + count // 2) % count
+        return (n, n) if self.in_order else (n, n + 1 - 2 * (n % 2))
+
+    def start(self, ks):
+        for k in ks:
+            for way in range(2):
+                self.go(self.ring_copy(way, 1, k, self.chunks[k][1], self.z))
+            self.go(self.core_copy(0, k, self.chunks[k][1], self.z, self.c))
 
     def first(self, ns=None):
         ns = range(len(self.chunks)) if ns is None else ns
@@ -83,10 +88,10 @@
 
     def step(self, s, ns=None):
         for n in range(len(self.chunks)) if ns is None else ns:
-            far = n < len(self.chunks) // 2
-            if s == 4 and not far:
-                continue
             for way, k in enumerate(self.turn(n)):
+                far = k % 2 == way
+                if s == 4 and not far:
+                    continue
                 zb = at_z(self.z, -s if way == 0 else s)
                 here = self.spot(k, zb, self.c)
                 self.ring_copy(way, s, k, here, zb).wait_recv()
@@ -420,15 +425,14 @@
     ring.step(3, [0])
     for line in lines:
         line.two()
-    pl.loop(3, 4)(project)
+    pl.loop(3, 5)(project)
     ring.step(3, [1])
     for p in pages:
         p.five()
-    pl.loop(4, 5)(project)
+    pl.loop(5, 7)(project)
+    ring.step(4)
     pl.loop(0, NREQ)(prefix)
-    pl.loop(5, 6)(project)
-    ring.step(4)
-    pl.loop(6, 8)(project)
+    pl.loop(7, 8)(project)
     for line in lines:
         line.three()
     for part in [ring, oring] + planes + lines:
@@ -488,9 +492,10 @@
 
         total = acc[...]
         result = total / pltpu.roll(total, HW, 1)
-        for b in range(2):
-            top, bottom = result[b * 128:b * 128 + 64], result[b * 128 + 64:b * 128 + 128]
-            out_ref[2 * i + b] = jnp.where(lanes((64, 128)) >= HW, top, pltpu.roll(bottom, HW, 1)).astype(BF16)
+        for b in range(4):
+            top, bottom = result[b * 64:b * 64 + 32], result[b * 64 + 32:b * 64 + 64]
+            out_ref[2 * i + b // 2, b % 2] = jnp.where(
+                lanes((32, 128)) >= HW, top, pltpu.roll(bottom, HW, 1)).astype(BF16)
 
 
 def renorm(v):
@@ -504,15 +509,21 @@
     greet([(dp, (t + n) % NT) for n in range(1, NT)])
     started = []
     order = [8, 9, 7, 10, 6, 11, 5, 12, 4, 13, 3, 14, 2, 15, 1]
-    for n in order:
-        to = (t + n) % NT
-        copy = pltpu.make_async_remote_copy(
-            src_ref=attn_ref.at[to], dst_ref=heads.at[t], send_sem=asend.at[n], recv_sem=arecv.at[n],
-            device_id=(dp, to), device_id_type=MESH)
-        copy.start()
-        started.append(copy)
-    own = pltpu.make_async_copy(attn_ref.at[t], heads.at[t], local.at[11])
-    own.start()
+
+    def exchange(half, n, to, origin):
+        return pltpu.make_async_remote_copy(
+            src_ref=attn_ref.at[to, half], dst_ref=heads.at[half, origin], send_sem=asend.at[half, n],
+            recv_sem=arecv.at[half, n], device_id=(dp, to), device_id_type=MESH)
+
+    for half in range(2):
+        for n in order:
+            copy = exchange(half, n, (t + n) % NT, t)
+            copy.start()
+            started.append(copy)
+    owns = [pltpu.make_async_copy(attn_ref.at[t, half], heads.at[half, t], local.at[11 + half])
+            for half in range(2)]
+    for own in owns:
+        own.start()
     eighths = [(part, j) for part in range(2) for j in range(4)]
 
     def place_in(part, j, core):
@@ -533,29 +544,31 @@
     loads = [pltpu.make_async_copy(a, b, local.at[n]) for n, (a, b) in enumerate(moves)]
     for copy in loads:
         copy.start()
-    base = h_ref[...].astype(F32)
-    own.wait()
-    for n in order:
-        frm = (t + NT - n) % NT
-        pltpu.make_async_remote_copy(
-            src_ref=attn_ref.at[t], dst_ref=heads.at[frm], send_sem=asend.at[n], recv_sem=arecv.at[n],
-            device_id=(dp, frm), device_id_type=MESH).wait_recv()
-    high = lanes((64, 128)) >= HW
-    for j in range(NT // 2):
-        even, odd = heads[2 * j].astype(F32), heads[2 * j + 1].astype(F32)
-        cols = slice(128 * j, 128 * j + 128)
-        lhs[0:64, cols] = jnp.where(high, odd, pltpu.roll(even, HW, 1)).astype(BF16)
-        lhs[64:128, cols] = jnp.where(high, pltpu.roll(odd, HW, 1), even).astype(BF16)
-    for n in range(8):
-        loads[n].wait()
-        matrix_copy(n, 1 - c).wait_recv()
-    attn_sum = jnp.dot(lhs[...], om[...].reshape(NT * HW, D), preferred_element_type=F32)
     rate = ra_ref[...].reshape(1, D)
-    mine = renorm(base + rate * (renorm(attn_sum) - base)).astype(BF16)
-    mixed[t] = mine
-    ring = Ring([(slab(mixed, 32 * k, 32), mixed.at[t, pl.ds(32 * k, 32)]) for k in range(4)], zsend, zrecv, psend, precv)
-    ring.first()
-    mixed_out[...] = mine
+    high = lanes((32, 128)) >= HW
+    ring = Ring([(slab(mixed, 32 * k, 32), mixed.at[t, pl.ds(32 * k, 32)]) for k in range(4)],
+                zsend, zrecv, psend, precv, in_order=True)
+    for half in range(2):
+        owns[half].wait()
+        for n in order:
+            frm = (t + NT - n) % NT
+            exchange(half, n, t, frm).wait_recv()
+        for j in range(NT // 2):
+            even, odd = heads[half, 2 * j].astype(F32), heads[half, 2 * j + 1].astype(F32)
+            cols = slice(128 * j, 128 * j + 128)
+            lhs[0:32, cols] = jnp.where(high, odd, pltpu.roll(even, HW, 1)).astype(BF16)
+            lhs[32:64, cols] = jnp.where(high, pltpu.roll(odd, HW, 1), even).astype(BF16)
+        if half == 0:
+            for n in range(8):
+                loads[n].wait()
+                matrix_copy(n, 1 - c).wait_recv()
+        attn_sum = jnp.dot(lhs[...], om[...].reshape(NT * HW, D), preferred_element_type=F32)
+        rows = slice(64 * half, 64 * half + 64)
+        base = h_ref[rows, :].astype(F32)
+        mine = renorm(base + rate * (renorm(attn_sum) - base)).astype(BF16)
+        mixed[t, rows] = mine
+        ring.start([2 * half, 2 * half + 1])
+        mixed_out[rows, :] = mine
     for copy in loads[8:]:
         copy.wait()
     scale_up, scale_gate = su_ref[...].reshape(1, 320), sg_ref[...].reshape(1, 320)
@@ -590,7 +603,7 @@
     def pass_on(d, near, far):
         for n in ([2, 3] if near else []) + ([0, 1] if far else []):
             for way in range(2):
-                k = (n + 2 * way) % 4
+                k = way + 2 * n if n < 2 else 1 - way + 2 * (n - 2)
                 rows = pl.ds(32 * k, 32)
                 recv, sent = (rr, sr) if way == 0 else (rl, sl)
                 value = local_sum(at_z(z, d if way == 0 else -d), k)
@@ -614,9 +627,9 @@
     pl.loop(3, 5)(feed)
     ring.step(3)
     pl.loop(5, 7)(feed)
+    ring.step(4)
     swapped(3)
     pass_on(3, True, False)
-    ring.step(4)
     pl.loop(7, 8)(feed)
     swapped(4)
     pass_on(4, False, True)
@@ -695,7 +708,7 @@
       lengths, *[far(a) for a in (request_adapter, request_prompt, prompt_page_table.T)])
     attn = pl.pallas_call(
         attend_kernel,
-        out_shape=pltpu.VMEM((NT, 64, 128), BF16),
+        out_shape=pltpu.VMEM((NT, 2, 32, 128), BF16),
         in_specs=[VM, VM, SM],
         out_specs=VM,
         scratch_shapes=[pltpu.VMEM((256, 128), F32), pltpu.SMEM((2 * NREQ,), jnp.int32)],
@@ -708,8 +721,8 @@
         in_specs=[VM, VM, VM, HB, HB, HB, VM, VM, VM],
         out_specs=(VM, VM),
         scratch_shapes=[
-            pltpu.VMEM((NT, 64, 128), BF16),
-            pltpu.VMEM((ROWS, NT * HW), BF16),
+            pltpu.VMEM((2, NT, 32, 128), BF16),
+            pltpu.VMEM((64, NT * HW), BF16),
             pltpu.VMEM((NZ, 2, 4, 16, D), BF16),
             pltpu.VMEM((320, D), BF16),
             pltpu.VMEM((320, D), BF16),
@@ -719,9 +732,9 @@
             pltpu.VMEM((NZ, ROWS, D), BF16),
             pltpu.VMEM((4, ROWS, D), BF16), pltpu.VMEM((4, ROWS, D), BF16),
             pltpu.VMEM((4, ROWS, D), BF16), pltpu.VMEM((4, ROWS, D), BF16),
-            DMA((16,)), DMA((16,)), DMA((8,)), DMA((8,)),
+            DMA((2, 16)), DMA((2, 16)), DMA((8,)), DMA((8,)),
             DMA((2, 4, 4)), DMA((2, 4, 4)), DMA((8, 4)), DMA((8, 4)),
-            DMA((8,)), DMA((8,)), DMA((2, 4, 4)), DMA((2, 4, 4)), DMA((12,)),
+            DMA((8,)), DMA((8,)), DMA((2, 4, 4)), DMA((2, 4, 4)), DMA((13,)),
         ],
         compiler_params=pltpu.CompilerParams(
             collective_id=1, has_side_effects=True, vmem_limit_bytes=44 * 2**20),

time: 129 us -> 128 us (level)
    pallas_call x1, Pallas kernels: 73.2 us -> 71.1 us  [local(): pl.pallas_call(mix_kernel, out_shape=(pltpu.VMEM((ROWS, D), F32), pltpu.V...]
where the time goes in v5:
time: 128 us
  Pallas kernels  128 us (100%)
    pallas_call x1, Pallas kernels, local(): pl.pallas_call(mix_kernel, out_shape=(pltpu.VMEM((ROWS, D), F32), pltpu.V...  71.1 us
    pallas_call x1, Pallas kernels, local(): pl.pallas_call(gather_kernel, out_shape=(pltpu.VMEM((GROUP, 128), BF16),...  44.9 us
    pallas_call x1, Pallas kernels, local(): pl.pallas_call(attend_kernel, out_shape=pltpu.VMEM((NT, 2, 32, 128), BF16...  10.4 us

profile of v5, /device:TPU:1, one launch (start us, length us, event | category | flops | bytes accessed | tf_op | source)
XLA Modules:
  0.0 127.7 jit_solution(6621220286878568747)
XLA Ops:
  0.0 0.0 copy-start
  0.0 0.0 copy-start.3
  0.0 0.0 copy-start.7
  0.0 0.0 copy-start.6
  0.0 0.0 copy-start.2
  0.0 0.0 copy-start.1
  0.0 0.0 copy-start.4
  0.0 44.9 %gather_project.1 = (bf16[2048,128]{1,0:T(8,128)(2,1)S(1)}, bf16[4096,128]{1,0:T(8,128)(2,1)S(1)}, bf16[2,4,8,2,16,640]{5,4,3,2,1,0:T(8,128)(2,1)S(1)}) custom-call(bf16[128,1280]{1,0:T(8,128)(2,1)} %h_ref.3, bf16[64,1280]{1,0:T(8,128)(2,1)} %o_ref.1, bf16[4,64,128]{2,1,0:T(8,128)(2,1)} %pg_ref.1, bf16[4,16,192]{2,1,0:T(8,128)(2,1)} %up_ref.1, ...), custom_call_target="tpu_custom_call" | custom-call | tf_op jit(solution)/shard_map/gather_project/pallas_call | solution.py:679
  45.0 10.4 %attend.1.attn_ref = bf16[16,2,32,128]{3,2,1,0:T(8,128)(2,1)S(1)} custom-call(bf16[2048,128]{1,0:T(8,128)(2,1)S(1)} %get-tuple-element.10.q_ref, bf16[4096,128]{1,0:T(8,128)(2,1)S(1)} %get-tuple-element.11.kv_ref, s32[1,8]{1,0:T(1,128)} %len_ref.3), custom_call_target="tpu_custom_call" | custom-call | tf_op jit(solution)/shard_map/attend/pallas_call | solution.py:709
  55.4 0.0 copy-done
  55.4 0.0 copy-done.3
  55.4 0.0 copy-done.7
  55.4 0.0 copy-done.6
  55.4 0.0 copy-done.2
  55.5 0.0 copy-done.1
  55.5 0.0 copy-done.4
  55.5 0.0 copy-start.5
  55.5 71.1 %mix_feed.1 = (f32[128,1280]{1,0:T(8,128)S(1)}, bf16[128,1280]{1,0:T(8,128)(2,1)S(1)}) custom-call(bf16[16,2,32,128]{3,2,1,0:T(8,128)(2,1)S(1)} %attend.1.attn_ref, bf16[2,4,8,2,16,640]{5,4,3,2,1,0:T(8,128)(2,1)S(1)} %get-tuple-element.12.o_ref, bf16[128,1280]{1,0:T(8,128)(2,1)S(1)} %copy-done, bf16[320,1280]{1,0:T(8,128)(2,1)S(1)} %bitcast.5, ...), custom_call_target="tpu_custom_call" | custom-call | tf_op jit(solution)/shard_map/mix_feed/pallas_call | solution.py:718
  126.6 0.0 copy-done.5
  126.6 1.1 finish.1
Async XLA Ops:
  0.0 55.4 %copy-start = (bf16[128,1280]{1,0:T(8,128)(2,1)S(1)}, bf16[128,1280]{1,0:T(8,128)(2,1)}, u32[]{:S(2)}) copy-start(bf16[128,1280]{1,0:T(8,128)(2,1)} %h_ref.3) | copy-start | bytes 983044
  0.0 55.4 %copy-start.3 = (bf16[320,1280]{1,0:T(8,128)(2,1)S(1)}, bf16[320,1280]{1,0:T(8,128)(2,1)}, u32[]{:S(2)}) copy-start(bf16[320,1280]{1,0:T(8,128)(2,1)} %wd_ref.1) | copy-start | bytes 2457604
  0.0 55.4 %copy-start.7 = (f32[320]{0:T(512)S(1)}, f32[320]{0:T(512)}, u32[]{:S(2)}) copy-start(f32[320]{0:T(512)} %sg_ref.1) | copy-start | bytes 3844
  0.0 55.4 %copy-start.6 = (f32[320]{0:T(512)S(1)}, f32[320]{0:T(512)}, u32[]{:S(2)}) copy-start(f32[320]{0:T(512)} %su_ref.1) | copy-start | bytes 3844
  0.0 55.4 %copy-start.2 = (bf16[1280,320]{0,1:T(8,128)(2,1)S(1)}, bf16[1280,320]{0,1:T(8,128)(2,1)}, u32[]{:S(2)}) copy-start(bf16[1280,320]{0,1:T(8,128)(2,1)} %param.31) | copy-start | bytes 2457604
  0.0 55.4 %copy-start.1 = (bf16[1280,320]{0,1:T(8,128)(2,1)S(1)}, bf16[1280,320]{0,1:T(8,128)(2,1)}, u32[]{:S(2)}) copy-start(bf16[1280,320]{0,1:T(8,128)(2,1)} %param.30) | copy-start | bytes 2457604
  0.0 55.4 %copy-start.4 = (f32[1280]{0:T(1024)S(1)}, f32[1280]{0:T(1024)}, u32[]{:S(2)}) copy-start(f32[1280]{0:T(1024)} %ra_ref.3) | copy-start | bytes 15364
  55.5 71.1 %copy-start.5 = (f32[1280]{0:T(1024)S(1)}, f32[1280]{0:T(1024)}, u32[]{:S(2)}) copy-start(f32[1280]{0:T(1024)} %rate_ref.1) | copy-start | bytes 15364

commit v6 on v5

--- a/solution.py
+++ b/solution.py
@@ -264,7 +264,7 @@
 
 def gather_kernel(h_ref, o_ref, pg_ref, up_ref, dn_ref, w_ref, gain_ref, len_ref, ra_ref, rp_ref, pt_ref,
                   q_out, kv_out, ob,
-                  gh, pb, ub, db, wide, sel, tail, su, gains, trig,
+                  gh, pb, ub, db, wide, sel, tail, su, gains, cosines, sines, mine,
                   zsend, zrecv, psend, precv, usend, urecv, xsend, xrecv, lsend, lrecv, local, dsend, drecv):
     dp, t, z, c = place()
     x, y = dp // 4, dp % 4
@@ -273,7 +273,7 @@
         (((x + 1) % 4) * 4 + y, t), (((x + 3) % 4) * 4 + y, t),
         (x * 4 + (y + 1) % 4, t), (x * 4 + (y + 3) % 4, t),
     ])
-    ring = Ring([(slab(gh, 64 * k, 64), h_ref.at[pl.ds(64 * k, 64)]) for k in range(2)],
+    ring = Ring([(slab(gh, 32 * k, 32), h_ref.at[pl.ds(32 * k, 32)]) for k in range(4)],
                 zsend, zrecv, psend, precv)
     quarters = [(x, o_ref.at[pl.ds(pl.multiple_of(16 * x, 16), 16), pl.ds(0, D // 2)]),
                 (y, o_ref.at[pl.ds(pl.multiple_of(16 * y, 16), 16), pl.ds(D // 2, D // 2)])]
@@ -288,7 +288,7 @@
         pages.append(Plane(4 + half, half, pg_ref.at[pl.ds(2 * half, 2)], pb.at[half], xsend, xrecv, local))
     planes = adapters + pages
     oring.first()
-    ring.first([0])
+    ring.first([0, 1])
     for p in planes:
         p.one()
     owns = [pltpu.make_async_copy(h_ref, gh.at[t], local.at[6])]
@@ -301,7 +301,7 @@
     for own in owns:
         own.start()
     oring.step(1)
-    ring.first([1])
+    ring.first([2, 3])
     for p in planes:
         p.two()
     for p in adapters:
@@ -310,7 +310,7 @@
     for own in owns:
         own.wait()
     oring.step(2)
-    ring.step(1, [0])
+    ring.step(1, [0, 1])
 
     lane = lanes((256, 128))
     low = lane < HW
@@ -323,15 +323,19 @@
     quarter = jnp.where(low, 0.0, 0.5 * math.pi)
 
     def waves(b):
-        rows, _, start = row_starts(len_ref, b * 256, (256, 128))
+        rows, req, start = row_starts(len_ref, b * 256, (256, 128))
         angle = (rows - start + PREFIX).astype(F32) * frequency
-        trig[b] = jnp.cos(angle - quarter)
+        wave = jnp.cos(angle - quarter)
+        cosines[b] = jnp.where(low, wave, 1.0)
+        sine = pltpu.roll(wave, HW, 1)
+        sines[b] = jnp.where(lane < 32, -sine, jnp.where(low, sine, 0.0))
+        mine[b] = jnp.where(lane // RANK == req, 1.0, 0.0).astype(BF16)
 
     pl.loop(0, 4)(waves)
     for p in pages:
         p.three()
     oring.step(3)
-    ring.step(1, [1])
+    ring.step(1, [2, 3])
     for p in adapters:
         p.four()
     for p in pages:
@@ -355,7 +359,7 @@
     oring.step(4)
     for line in lines:
         line.one()
-    ring.step(2, [0])
+    ring.step(2, [0, 1])
 
     def unit(v):
         total = jnp.sum(jnp.where(low, v * v, 0.0), axis=1, keepdims=True)
@@ -397,14 +401,10 @@
         ring.from_core(i)
         zb = at_z(z, delta(i))
         values = gh[pl.ds(zb * 2, 2)].reshape(256, D)
-        _, req, _ = row_starts(len_ref, zb * 256, (256, 128))
         every = lax.dot_general(values, wide[...], NT_DIMS, preferred_element_type=F32)
-        middle = jnp.where(lane // RANK == req, every[:, 0:128], 0.0).astype(BF16)
+        middle = every[:, 0:128].astype(BF16) * mine[zb]
         both = every[:, 128:384] + 0.5 * jnp.dot(middle, su[...], preferred_element_type=F32)
-        wave = trig[zb]
-        cosine = jnp.where(low, wave, 1.0)
-        sine = pltpu.roll(wave, HW, 1)
-        sine = jnp.where(lane < 32, -sine, jnp.where(low, sine, 0.0))
+        cosine, sine = cosines[zb], sines[zb]
 
         def rotate(v):
             other = jnp.where(lane < 32, pltpu.roll(v, 96, 1), pltpu.roll(v, 32, 1))
@@ -417,16 +417,16 @@
             low, unit(rotate(key_value)), key_value).astype(BF16)
 
     pl.loop(0, 1)(project)
-    ring.step(2, [1])
+    ring.step(2, [2, 3])
     pl.loop(1, 2)(project)
     for p in pages:
         p.four()
     pl.loop(2, 3)(project)
-    ring.step(3, [0])
+    ring.step(3, [0, 1])
     for line in lines:
         line.two()
     pl.loop(3, 5)(project)
-    ring.step(3, [1])
+    ring.step(3, [2, 3])
     for p in pages:
         p.five()
     pl.loop(5, 7)(project)
@@ -502,7 +502,7 @@
     return v * lax.rsqrt(jnp.mean(v * v, axis=-1, keepdims=True) + EPS)
 
 
-def mix_kernel(attn_ref, o_ref, h_ref, wu_ref, wg_ref, wd_ref, su_ref, sg_ref, ra_ref, sum_out, mixed_out,
+def mix_kernel(attn_ref, o_ref, h_ref, wu_ref, wg_ref, wd_ref, su_ref, sg_ref, ra_ref, rf_ref, rows_out,
                heads, lhs, om, wu, wg, wd, mixed, part, peer, rr, rl, sr, sl,
                asend, arecv, msend, mrecv, zsend, zrecv, psend, precv, qsend, qrecv, rsend, rrecv, local):
     dp, t, z, c = place()
@@ -568,7 +568,6 @@
         mine = renorm(base + rate * (renorm(attn_sum) - base)).astype(BF16)
         mixed[t, rows] = mine
         ring.start([2 * half, 2 * half + 1])
-        mixed_out[rows, :] = mine
     for copy in loads[8:]:
         copy.wait()
     scale_up, scale_gate = su_ref[...].reshape(1, 320), sg_ref[...].reshape(1, 320)
@@ -639,12 +638,15 @@
     swapped(1)
     pass_on(1, True, True)
     swap(0, z).wait_recv()
+    last_rate = rf_ref[...].reshape(1, D)
     for k in range(4):
         rows = pl.ds(32 * k, 32)
         value = local_sum(z, k)
         for way in range(2):
             rs_copy(way, 1, k, (sr if way == 0 else sl).at[0, rows]).wait_recv()
-        sum_out[rows, :] = value + rr[0, rows].astype(F32) + rl[0, rows].astype(F32)
+        value = value + rr[0, rows].astype(F32) + rl[0, rows].astype(F32)
+        base = mixed[t, rows].astype(F32)
+        rows_out[rows, :] = renorm(base + last_rate * (renorm(value) - base)).astype(BF16)
     ring.drain()
     for copy in started:
         copy.wait_send()
@@ -652,10 +654,10 @@
         swap(i, at_z(z, delta(i))).wait_send()
 
 
-def finish_kernel(sum_ref, mixed_ref, rate_ref, out_ref):
-    base = mixed_ref[...].astype(F32)
-    rate = rate_ref[...].reshape(1, D)
-    out_ref[...] = renorm(base + rate * (renorm(sum_ref[...]) - base)).astype(BF16)
+def finish_kernel(rows_ref, out_ref, sem):
+    copy = pltpu.make_async_copy(rows_ref, out_ref, sem)
+    copy.start()
+    copy.wait()
 
 
 VM = pl.BlockSpec(memory_space=pltpu.VMEM)
@@ -696,7 +698,9 @@
             pltpu.VMEM((128, 256), BF16),
             pltpu.VMEM((8, 128), F32),
             pltpu.VMEM((NZ, 256, 128), F32),
-            DMA((2, 4, 2)), DMA((2, 4, 2)), DMA((8, 2)), DMA((8, 2)), DMA((2, 4, 2)), DMA((2, 4, 2)),
+            pltpu.VMEM((NZ, 256, 128), F32),
+            pltpu.VMEM((NZ, 256, 128), BF16),
+            DMA((2, 4, 4)), DMA((2, 4, 4)), DMA((8, 4)), DMA((8, 4)), DMA((2, 4, 2)), DMA((2, 4, 2)),
             DMA((6, 8)), DMA((6, 8)), DMA((2, 4)), DMA((2, 4)), DMA((11,)), DMA((2,)), DMA((2,)),
         ],
         compiler_params=pltpu.CompilerParams(
@@ -715,11 +719,11 @@
         compiler_params=pltpu.CompilerParams(vmem_limit_bytes=16 * 2**20),
         name="attend",
     )(stay(queries), stay(key_values), lengths)
-    sums, mixed = pl.pallas_call(
+    rows = pl.pallas_call(
         mix_kernel,
-        out_shape=(pltpu.VMEM((ROWS, D), F32), pltpu.VMEM((ROWS, D), BF16)),
-        in_specs=[VM, VM, VM, HB, HB, HB, VM, VM, VM],
-        out_specs=(VM, VM),
+        out_shape=pltpu.VMEM((ROWS, D), BF16),
+        in_specs=[VM, VM, VM, HB, HB, HB, VM, VM, VM, VM],
+        out_specs=VM,
         scratch_shapes=[
             pltpu.VMEM((2, NT, 32, 128), BF16),
             pltpu.VMEM((64, NT * HW), BF16),
@@ -740,15 +744,16 @@
             collective_id=1, has_side_effects=True, vmem_limit_bytes=44 * 2**20),
         name="mix_feed",
     )(stay(attn), stay(matrix), hidden, up_matrix.T, gate_matrix.T, down_matrix,
-      up_scaling, gate_scaling, attention_rate)
+      up_scaling, gate_scaling, attention_rate, feedforward_rate)
     return pl.pallas_call(
         finish_kernel,
         out_shape=jax.ShapeDtypeStruct((ROWS, D), BF16),
-        in_specs=[VM, VM, VM],
-        out_specs=VM,
+        in_specs=[VM],
+        out_specs=HB,
+        scratch_shapes=[DMA],
         compiler_params=pltpu.CompilerParams(vmem_limit_bytes=16 * 2**20),
         name="finish",
-    )(stay(sums), stay(mixed), feedforward_rate)
+    )(stay(rows))
 
 
 def solution(mesh):

time: 128 us -> 127 us (level)
  Pallas kernels: 128 us -> 126 us
    pallas_call x1, Pallas kernels: 71.1 us -> 69.4 us  [local(): pl.pallas_call(mix_kernel, out_shape=pltpu.VMEM((ROWS, D), BF16), in_spec...]
    pallas_call x1, Pallas kernels: 44.9 us -> 46.3 us  [local(): pl.pallas_call(gather_kernel, out_shape=(pltpu.VMEM((GROUP, 128), BF16),...]
where the time goes in v6:
time: 127 us; the launch traced here: 126 us
  Pallas kernels  126 us (99%)
    pallas_call x1, Pallas kernels, local(): pl.pallas_call(mix_kernel, out_shape=pltpu.VMEM((ROWS, D), BF16), in_spec...  69.4 us
    pallas_call x1, Pallas kernels, local(): pl.pallas_call(gather_kernel, out_shape=(pltpu.VMEM((GROUP, 128), BF16),...  46.3 us
    pallas_call x1, Pallas kernels, local(): pl.pallas_call(attend_kernel, out_shape=pltpu.VMEM((NT, 2, 32, 128), BF16...  9.63 us

profile of v6, /device:TPU:1, one launch (start us, length us, event | category | flops | bytes accessed | tf_op | source)
XLA Modules:
  0.0 126.4 jit_solution(1614867596809020510)
XLA Ops:
  0.0 0.0 copy-start
  0.0 0.0 copy-start.5
  0.0 0.0 copy-start.3
  0.0 0.0 copy-start.7
  0.0 0.0 copy-start.6
  0.0 0.0 copy-start.2
  0.0 0.0 copy-start.1
  0.0 0.0 copy-start.4
  0.1 46.3 %gather_project.1 = (bf16[2048,128]{1,0:T(8,128)(2,1)S(1)}, bf16[4096,128]{1,0:T(8,128)(2,1)S(1)}, bf16[2,4,8,2,16,640]{5,4,3,2,1,0:T(8,128)(2,1)S(1)}) custom-call(bf16[128,1280]{1,0:T(8,128)(2,1)} %h_ref.3, bf16[64,1280]{1,0:T(8,128)(2,1)} %o_ref.1, bf16[4,64,128]{2,1,0:T(8,128)(2,1)} %pg_ref.1, bf16[4,16,192]{2,1,0:T(8,128)(2,1)} %up_ref.1, ...), custom_call_target="tpu_custom_call" | custom-call | tf_op jit(solution)/shard_map/gather_project/pallas_call | solution.py:681
  46.4 9.6 %attend.1.attn_ref = bf16[16,2,32,128]{3,2,1,0:T(8,128)(2,1)S(1)} custom-call(bf16[2048,128]{1,0:T(8,128)(2,1)S(1)} %get-tuple-element.8.q_ref, bf16[4096,128]{1,0:T(8,128)(2,1)S(1)} %get-tuple-element.9.kv_ref, s32[1,8]{1,0:T(1,128)} %len_ref.3), custom_call_target="tpu_custom_call" | custom-call | tf_op jit(solution)/shard_map/attend/pallas_call | solution.py:713
  56.0 0.0 copy-done
  56.0 0.0 copy-done.5
  56.0 0.0 copy-done.3
  56.0 0.0 copy-done.7
  56.0 0.0 copy-done.6
  56.0 0.0 copy-done.2
  56.0 0.0 copy-done.1
  56.1 0.0 copy-done.4
  56.1 69.4 %mix_feed.1.rows_ref = bf16[128,1280]{1,0:T(8,128)(2,1)S(1)} custom-call(bf16[16,2,32,128]{3,2,1,0:T(8,128)(2,1)S(1)} %attend.1.attn_ref, bf16[2,4,8,2,16,640]{5,4,3,2,1,0:T(8,128)(2,1)S(1)} %get-tuple-element.10.o_ref, bf16[128,1280]{1,0:T(8,128)(2,1)S(1)} %copy-done, bf16[320,1280]{1,0:T(8,128)(2,1)S(1)} %bitcast.5, bf16[320,1280]{1,0:T(8,128)(2,1)S(1)} %bitcast.6, ...), custom_call_target="tpu_custom_call" | custom-call | tf_op jit(solution)/shard_map/mix_feed/pallas_call | solution.py:722
  125.5 0.7 finish.1
Async XLA Ops:
  0.0 56.0 %copy-start = (bf16[128,1280]{1,0:T(8,128)(2,1)S(1)}, bf16[128,1280]{1,0:T(8,128)(2,1)}, u32[]{:S(2)}) copy-start(bf16[128,1280]{1,0:T(8,128)(2,1)} %h_ref.3) | copy-start | bytes 983044
  0.0 56.0 %copy-start.5 = (f32[1280]{0:T(1024)S(1)}, f32[1280]{0:T(1024)}, u32[]{:S(2)}) copy-start(f32[1280]{0:T(1024)} %rf_ref.1) | copy-start | bytes 15364
  0.0 56.0 %copy-start.3 = (bf16[320,1280]{1,0:T(8,128)(2,1)S(1)}, bf16[320,1280]{1,0:T(8,128)(2,1)}, u32[]{:S(2)}) copy-start(bf16[320,1280]{1,0:T(8,128)(2,1)} %wd_ref.1) | copy-start | bytes 2457604
  0.0 56.0 %copy-start.7 = (f32[320]{0:T(512)S(1)}, f32[320]{0:T(512)}, u32[]{:S(2)}) copy-start(f32[320]{0:T(512)} %sg_ref.1) | copy-start | bytes 3844
  0.0 56.0 %copy-start.6 = (f32[320]{0:T(512)S(1)}, f32[320]{0:T(512)}, u32[]{:S(2)}) copy-start(f32[320]{0:T(512)} %su_ref.1) | copy-start | bytes 3844
  0.0 56.0 %copy-start.2 = (bf16[1280,320]{0,1:T(8,128)(2,1)S(1)}, bf16[1280,320]{0,1:T(8,128)(2,1)}, u32[]{:S(2)}) copy-start(bf16[1280,320]{0,1:T(8,128)(2,1)} %param.31) | copy-start | bytes 2457604
  0.0 56.0 %copy-start.1 = (bf16[1280,320]{0,1:T(8,128)(2,1)S(1)}, bf16[1280,320]{0,1:T(8,128)(2,1)}, u32[]{:S(2)}) copy-start(bf16[1280,320]{0,1:T(8,128)(2,1)} %param.30) | copy-start | bytes 2457604
  0.0 56.0 %copy-start.4 = (f32[1280]{0:T(1024)S(1)}, f32[1280]{0:T(1024)}, u32[]{:S(2)}) copy-start(f32[1280]{0:T(1024)} %ra_ref.3) | copy-start | bytes 15364
